TPU v7x, 32 devices: a whole 2x2x4 slice. The times are simulated.
32 devices in a mesh: wave: 8 (over z, y), lev: 4 (over x, core).
Axes of the slice: x: 2, y: 2, z: 4, core: 2. Of those that a mesh axis runs over, the one named last changes fastest.
Arguments:
- spectral: float32 [8, 136, 2, 1280], P('wave', 'lev'), may hold values from -6 to 6
- to_modes: float32 [136, 136], replicated
- from_modes: float32 [136, 136], replicated
- mode_depths: float32 [136], replicated, may hold values from 0.05 to 5
- legendre: float32 [8, 16, 1280], P('wave'), may hold values from -0.03125 to 0.03125
- wave_ids: int32 [8], replicated, may hold values from 0 to 1279, as said below
- lat_points: int32 [16], P('wave'), may hold values from 20 to 5136, as said below
Outputs:
- grid: float32 [136, 16, 5136], P('lev', 'wave')
Inputs may be any that keep to these rules, and one draw needn't show every extreme that they name: `wave_ids`: distinct and ascending; 0 and 1279 are always among them. `lat_points`: each is 20 + 4 k for a whole k; not falling along the latitudes; the last is always 5136.
All inputs are finite; a program needn't handle non-finite values.
Results may differ from a plain program's by a relative error of at most 0.0003.
Values sent between devices are 32-bit elements; how exact they have to be, the bound alone decides.
No kernel may reach another device: no remote copies, remote signals or barrier semaphores. Data moves between devices by JAX's collectives and lax.ppermute only.
A program may use at most 64 MiB of HBM per device.

v0:
```python
import math

import jax
import jax.numpy as jnp
from jax import lax
from jax.sharding import PartitionSpec as P

LONS = 5136


two_pi = 2.0 * math.pi


def on_device(spectral, to_modes, from_modes, mode_depths, legendre, wave_ids, lat_points):
    highest = lax.Precision.HIGHEST
    waves_here = spectral.shape[0]
    total_orders = spectral.shape[3]
    block_len = total_orders // lax.axis_size("lev")
    columns = lax.all_to_all(spectral, "lev", split_axis=3, concat_axis=1, tiled=True)
    mode_coeffs = jnp.einsum("kl,wlcn->wkcn", to_modes, columns, precision=highest)
    first_order = lax.axis_index("lev") * block_len
    order_ids = first_order + jnp.arange(block_len)
    orders = order_ids.astype(jnp.float32)
    damping = 1.0 + mode_depths[:, None] * (orders * (orders + 1.0))[None, :] / float(
        total_orders * total_orders
    )
    divergence = jnp.einsum(
        "lk,wkcn->wlcn", from_modes, mode_coeffs / damping[None, :, None, :], precision=highest
    )
    own_ids = lax.dynamic_slice_in_dim(wave_ids, lax.axis_index("wave") * waves_here, waves_here)
    level_major = lax.all_to_all(divergence, "lev", split_axis=1, concat_axis=3, tiled=True)
    keep_mask = (jnp.arange(total_orders)[None, :] >= own_ids[:, None]).astype(jnp.float32)
    fourier = jnp.einsum(
        "wjn,wlcn->lwcj", legendre * keep_mask[:, None, :], level_major, precision=highest
    )
    band_data = lax.all_to_all(fourier, "wave", split_axis=3, concat_axis=1, tiled=True)
    positions = jnp.arange(LONS)

    def one_row(inputs):
        coeffs, points = inputs
        residue = wave_ids[:, None] * positions[None, :] % points
        phases = jnp.float32(two_pi) * residue.astype(jnp.float32) / points.astype(jnp.float32)
        weight = jnp.where(2 * wave_ids < points, jnp.where(wave_ids == 0, 1.0, 2.0), 0.0).astype(
            jnp.float32
        )
        basis_table = jnp.concatenate(
            [jnp.cos(phases) * weight[:, None], jnp.sin(phases) * weight[:, None]], 0
        )
        coefficient = jnp.concatenate([coeffs[:, :, 0], -coeffs[:, :, 1]], 1)
        lat_row = jnp.dot(coefficient, basis_table, precision=highest)
        return lat_row * (positions < points).astype(jnp.float32)[None, :]

    lat_rows = lax.map(one_row, (jnp.moveaxis(band_data, 3, 0), lat_points))
    return jnp.transpose(lat_rows, (1, 0, 2))


def solution(mesh):
    return jax.shard_map(
        on_device,
        mesh=mesh,
        in_specs=(
            P("wave", "lev", None, None),
            P(),
            P(),
            P(),
            P("wave", None, None),
            P(),
            P("wave"),
        ),
        out_specs=P("lev", "wave", None),
        check_vma=False,
    )
```

profile of v0, /device:TPU:0, one launch (start us, length us, event | category | flops | bytes accessed | tf_op | source)
XLA Modules:
  0.0 79.2 jit_solution(634367973494513038)
XLA Ops:
  0.0 2.6 %copy.29 = f32[1,34,2,1280]{1,2,0,3:T(2,128)S(1)} copy(f32[1,34,2,1280]{3,2,1,0:T(2,128)} %param.9) | data formatting | bytes 696320 | tf_op args[0]
  2.7 3.0 %reshape.90 = f32[4,1,21760]{2,1,0:T(1,128)} reshape(f32[1280,1,2,34]{3,2,1,0:T(2,128)S(1)} %bitcast.71) | data formatting | bytes 696320
  5.7 4.2 %all-to-all-start = ((f32[4,1,21760]{2,1,0:T(1,128)}), f32[4,1,21760]{2,1,0:T(1,128)S(1)}, u32[]{:S(2)}, u32[]{:S(2)}) async-start(f32[4,1,21760]{2,1,0:T(1,128)} %reshape.90), calls=%async_computation | async-start | bytes 696320 | tf_op jit(solution)/shard_map/all_to_all | solution.py:19
  10.0 6.9 %all-to-all-done = f32[4,1,21760]{2,1,0:T(1,128)S(1)} async-done(((f32[4,1,21760]{2,1,0:T(1,128)}), f32[4,1,21760]{2,1,0:T(1,128)S(1)}, u32[]{:S(2)}, u32[]{:S(2)}) %all-to-all-start) | async-done | bytes 348192 | tf_op jit(solution)/shard_map/all_to_all | solution.py:19
  17.4 1.6 %reduce = f32[4,21760]{1,0:T(4,128)S(1)} reduce(f32[4,1,21760]{2,1,0:T(1,128)S(1)} %all-to-all-done, f32[]{:T(128)} %broadcast.99), dimensions={1}, to_apply=%all_to_all.35.reduce_sub_computation | reduce | bytes 696324 | tf_op jit(solution)/shard_map/all_to_all | solution.py:19
  19.0 2.2 %reshape.91 = f32[1280,1,2,34]{3,2,1,0:T(2,128)S(1)} reshape(f32[4,21760]{1,0:T(4,128)S(1)} %reduce) | data formatting | bytes 696320
  21.3 1.3 %copy.30 = f32[1,34,2,4,320]{4,2,1,3,0:T(2,128)S(1)} copy(f32[1,34,2,4,320]{1,2,4,3,0:T(2,128)S(1)} %bitcast.70) | data formatting | bytes 696320 | tf_op jit(solution)/shard_map/all_to_all | solution.py:19
  23.6 1.0 %copy.32 = f32[1,136,2,320]{3,2,0,1:T(2,128)} copy(f32[1,136,2,320]{3,1,2,0:T(8,128)S(1)} %convolution_bitcast_fusion) | data formatting | bytes 696320 | tf_op jit(solution)/shard_map/lk,wkcn->wlcn/transpose | solution.py:27
  24.6 3.6 %all-to-all-start.1 = ((f32[1,136,2,320]{3,2,0,1:T(2,128)}), f32[1,136,2,320]{3,2,0,1:T(2,128)S(1)}, u32[]{:S(2)}, u32[]{:S(2)}) async-start(f32[1,136,2,320]{3,2,0,1:T(2,128)} %copy.32), calls=%async_computation.1 | async-start | bytes 835584 | tf_op jit(solution)/shard_map/all_to_all | solution.py:31
  29.5 6.4 %all-to-all-done.1 = f32[1,136,2,320]{3,2,0,1:T(2,128)S(1)} async-done(((f32[1,136,2,320]{3,2,0,1:T(2,128)}), f32[1,136,2,320]{3,2,0,1:T(2,128)S(1)}, u32[]{:S(2)}, u32[]{:S(2)}) %all-to-all-start.1) | async-done | bytes 348192 | tf_op jit(solution)/shard_map/all_to_all | solution.py:31
  36.3 0.8 convolution_bitcast_fusion.2
  37.1 0.7 reshape.92
  37.8 6.5 %all-to-all-start.2 = ((f32[8,1,136]{2,1,0:T(1,128)}), f32[8,1,136]{2,1,0:T(1,128)S(1)}, u32[]{:S(2)}, u32[]{:S(2)}) async-start(f32[8,1,136]{2,1,0:T(1,128)} %reshape.92), calls=%async_computation.2 | async-start | bytes 16384 | tf_op jit(solution)/shard_map/all_to_all | solution.py:36
  44.3 6.5 %all-to-all-done.2 = f32[8,1,136]{2,1,0:T(1,128)S(1)} async-done(((f32[8,1,136]{2,1,0:T(1,128)}), f32[8,1,136]{2,1,0:T(1,128)S(1)}, u32[]{:S(2)}, u32[]{:S(2)}) %all-to-all-start.2) | async-done | bytes 4384 | tf_op jit(solution)/shard_map/all_to_all | solution.py:36
  51.6 26.6 %while.12 = (s32[]{:T(128)}, f32[2,34,5136]{2,0,1:T(2,128)S(1)}, f32[2,34,8,2]{1,2,3,0:T(8,128)S(1)}, s32[8]{0:T(128)S(1)}, s32[2]{0:T(128)S(1)}, /*index=5*/s32[]{:T(128)}, s32[]{:T(128)}) while((s32[]{:T(128)}, f32[2,34,5136]{2,0,1:T(2,128)S(1)}, f32[2,34,8,2]{1,2,3,0:T(8,128)S(1)}, s32[8]{0:T(128)S(1)}, ...), condition=%wide.region_1.2_spmd.clone.clone, body=%wide.region_0.1_spmd.clone.clone.sunk | while | flops 34329884 | bytes 4202137 | solution.py:53
  54.8 2.3 %cosine_multiply_fusion.2 = (f32[8,5136]{1,0:T(8,128)S(1)}, f32[8,5136]{1,0:T(8,128)S(1)}) fusion(f32[8]{0:T(128)S(1)} %compare_select_fusion.3, f32[]{:T(128)S(6)} %convert_element_type.54, pred[]{:T(512)S(6)} %lt.78, s32[]{:T(128)S(6)} %select_n.59, s32[8]{0:T(128)S(1)} %get-tuple-element.139), kind=kLoop, calls=%fused_computation.15.clone.1 | loop fusion | flops 534144 | bytes 328777 | tf_op jit(solution)/shard_map/while/body/eval_jaxpr/mul | solution.py:47
  57.8 0.9 %fusion.38 = f32[1,34,5136]{2,1,0:T(8,128)S(1)} fusion(f32[5136]{0:T(1024)S(1)} %fusion.37, f32[8,5136]{1,0:T(8,128)S(1)} %get-tuple-element.118, f32[8,5136]{1,0:T(8,128)S(1)} %get-tuple-element.119, f32[34,8]{0,1:T(8,128)S(1)} %get-tuple-element.120, f32[34,8]{0,1:T(8,128)S(1)} %get-tuple-element.121), kind=kOutput, calls=%fused_computation.2.clone.1 | convolution fusion | flops 33785152 | bytes 1049920 | tf_op jit(solution)/shard_map/while/body/eval_jaxpr/dot_general | solution.py:50
  58.7 0.7 copy.49
  59.4 5.3 %dynamic_update_slice.7 = f32[2,34,5136]{2,0,1:T(2,128)S(1)} dynamic-update-slice(f32[2,34,5136]{2,0,1:T(2,128)S(1)} %get-tuple-element.130, f32[1,34,5136]{2,0,1:T(1,128)S(1)} %copy.49, s32[]{:T(128)} %get-tuple-element.129, s32[]{:T(128)} %constant.25.clone.1..sunk, s32[]{:T(128)} %constant.25.clone.1..sunk) | dynamic-update-slice | bytes 1396996 | tf_op jit(solution)/shard_map/while/body/jit(dynamic_update_index_in_dim)/dynamic_update_slice | solution.py:53
  68.0 2.3 %cosine_multiply_fusion.2 = (f32[8,5136]{1,0:T(8,128)S(1)}, f32[8,5136]{1,0:T(8,128)S(1)}) fusion(f32[8]{0:T(128)S(1)} %compare_select_fusion.3, f32[]{:T(128)S(6)} %convert_element_type.54, pred[]{:T(512)S(6)} %lt.78, s32[]{:T(128)S(6)} %select_n.59, s32[8]{0:T(128)S(1)} %get-tuple-element.139), kind=kLoop, calls=%fused_computation.15.clone.1 | loop fusion | flops 534144 | bytes 328777 | tf_op jit(solution)/shard_map/while/body/eval_jaxpr/mul | solution.py:47
  71.0 0.9 %fusion.38 = f32[1,34,5136]{2,1,0:T(8,128)S(1)} fusion(f32[5136]{0:T(1024)S(1)} %fusion.37, f32[8,5136]{1,0:T(8,128)S(1)} %get-tuple-element.118, f32[8,5136]{1,0:T(8,128)S(1)} %get-tuple-element.119, f32[34,8]{0,1:T(8,128)S(1)} %get-tuple-element.120, f32[34,8]{0,1:T(8,128)S(1)} %get-tuple-element.121), kind=kOutput, calls=%fused_computation.2.clone.1 | convolution fusion | flops 33785152 | bytes 1049920 | tf_op jit(solution)/shard_map/while/body/eval_jaxpr/dot_general | solution.py:50
  71.9 0.7 copy.49
  72.6 5.5 %dynamic_update_slice.7 = f32[2,34,5136]{2,0,1:T(2,128)S(1)} dynamic-update-slice(f32[2,34,5136]{2,0,1:T(2,128)S(1)} %get-tuple-element.130, f32[1,34,5136]{2,0,1:T(1,128)S(1)} %copy.49, s32[]{:T(128)} %get-tuple-element.129, s32[]{:T(128)} %constant.25.clone.1..sunk, s32[]{:T(128)} %constant.25.clone.1..sunk) | dynamic-update-slice | bytes 1396996 | tf_op jit(solution)/shard_map/while/body/jit(dynamic_update_index_in_dim)/dynamic_update_slice | solution.py:53
  78.1 1.1 %copy-done.5 = f32[2,34,5136]{2,0,1:T(2,128)} copy-done((f32[2,34,5136]{2,0,1:T(2,128)}, f32[2,34,5136]{2,0,1:T(2,128)S(1)}, u32[]{:S(2)}) %copy-start.5) | copy-done | bytes 1397016
  (37 shorter events, 7.9 us)
Async XLA Ops:
  0.0 22.5 %copy-start = (f32[136,136]{1,0:T(8,128)S(1)}, f32[136,136]{1,0:T(8,128)}, u32[]{:S(2)}) copy-start(f32[136,136]{1,0:T(8,128)} %param.10) | copy-start | bytes 221956
  2.6 7.3 %copy-start.4 = (f32[136]{0:T(256)S(1)}, f32[136]{0:T(256)}, u32[]{:S(2)}) copy-start(f32[136]{0:T(256)} %param.12) | copy-start | bytes 1636
  5.7 11.2 %all-to-all-start = ((f32[4,1,21760]{2,1,0:T(1,128)}), f32[4,1,21760]{2,1,0:T(1,128)S(1)}, u32[]{:S(2)}, u32[]{:S(2)}) async-start(f32[4,1,21760]{2,1,0:T(1,128)} %reshape.90), calls=%async_computation | async-start | bytes 696320 | tf_op jit(solution)/shard_map/all_to_all | solution.py:19
  21.3 1.8 %copy-start.1 = (f32[136,136]{1,0:T(8,128)S(1)}, f32[136,136]{1,0:T(8,128)}, u32[]{:S(2)}) copy-start(f32[136,136]{1,0:T(8,128)} %param.11) | copy-start | bytes 221956
  23.1 5.1 %copy-start.3 = (s32[8]{0:T(128)S(1)}, s32[8]{0:T(128)}, u32[]{:S(2)}) copy-start(s32[8]{0:T(128)} %param.14) | copy-start | bytes 100
  24.6 11.7 %copy-start.2 = (f32[1,16,1280]{2,1,0:T(8,128)S(1)}, f32[1,16,1280]{2,1,0:T(8,128)}, u32[]{:S(2)}) copy-start(f32[1,16,1280]{2,1,0:T(8,128)} %param.13) | copy-start | bytes 245764
  24.6 27.0 %copy-start.6 = (s32[2]{0:T(128)S(1)}, s32[2]{0:T(128)}, u32[]{:S(2)}) copy-start(s32[2]{0:T(128)} %param.15) | copy-start | bytes 28
  24.6 11.3 %all-to-all-start.1 = ((f32[1,136,2,320]{3,2,0,1:T(2,128)}), f32[1,136,2,320]{3,2,0,1:T(2,128)S(1)}, u32[]{:S(2)}, u32[]{:S(2)}) async-start(f32[1,136,2,320]{3,2,0,1:T(2,128)} %copy.32), calls=%async_computation.1 | async-start | bytes 835584 | tf_op jit(solution)/shard_map/all_to_all | solution.py:31
  37.8 13.0 %all-to-all-start.2 = ((f32[8,1,136]{2,1,0:T(1,128)}), f32[8,1,136]{2,1,0:T(1,128)S(1)}, u32[]{:S(2)}, u32[]{:S(2)}) async-start(f32[8,1,136]{2,1,0:T(1,128)} %reshape.92), calls=%async_computation.2 | async-start | bytes 16384 | tf_op jit(solution)/shard_map/all_to_all | solution.py:36
  78.1 1.1 %copy-start.5 = (f32[2,34,5136]{2,0,1:T(2,128)}, f32[2,34,5136]{2,0,1:T(2,128)S(1)}, u32[]{:S(2)}) copy-start(f32[2,34,5136]{2,0,1:T(2,128)S(1)} %get-tuple-element.40) | copy-start | bytes 4190980
where the time goes:
time: 79.7 us; the launch traced here: 79.2 us
  local copies, waits for them, and re-layouts  27.1 us (34%)
  waiting for transfers between devices  19.7 us (25%)
  starting transfers between devices  14.3 us (18%)
  other arithmetic  10.3 us (13%)
  loops' own time  4.04 us (5%)
  matrix products  3.55 us (4%)
    dynamic_update_slice x4, local copies, waits for them, and re-layouts, on_device(): lat_rows = lax.map(one_row, (jnp.moveaxis(band_data, 3, 0), lat_points))  12.3 us
    unnamed x19, local copies, waits for them, and re-layouts  9.8 us
    all_to_all x1, waiting for transfers between devices, on_device(): lax.all_to_all(spectral, 'lev', split_axis=3, concat_axis=1, tiled=True)  6.85 us
    all_to_all x1, waiting for transfers between devices, on_device(): lax.all_to_all(fourier, 'wave', split_axis=3, concat_axis=1, tiled=True)  6.51 us
    all_to_all x1, starting transfers between devices, on_device(): lax.all_to_all(fourier, 'wave', split_axis=3, concat_axis=1, tiled=True)  6.5 us
    all_to_all x1, waiting for transfers between devices, on_device(): lax.all_to_all(divergence, 'lev', split_axis=1, concat_axis=3, tiled=True)  6.37 us
    mul x2, other arithmetic, one_row(): jnp.cos(phases) * weight[:, None]  4.69 us
    all_to_all x1, starting transfers between devices, on_device(): lax.all_to_all(spectral, 'lev', split_axis=3, concat_axis=1, tiled=True)  4.21 us
  transfers between devices with their start and end apart: 3, of which 3 were waited for; matrix products, arithmetic and copies ran while one was open for 2% of the time, Pallas kernels for 0%

commit v1 on v0

v1 whole, which is shorter than its diff:
```python
import functools
import math

import jax
import jax.numpy as jnp
from jax import lax
from jax.experimental import pallas as pl
from jax.experimental.pallas import tpu as pltpu
from jax.sharding import PartitionSpec as P

LONS = 5136
F32, BF16 = jnp.float32, jnp.bfloat16


def split(x):
    hi = x.astype(BF16)
    return hi, (x - hi.astype(F32)).astype(BF16)


def dot3(a, b, contract):
    dot = functools.partial(
        lax.dot_general, dimension_numbers=(contract, ((), ())), preferred_element_type=F32
    )
    return dot(a[0], b[0]) + (dot(a[0], b[1]) + dot(a[1], b[0]))


def send_kernel(lev_devices, waves, ids_ref, spec_ref, to_ref, from_ref, depth_ref, leg_ref, out_ref, cols_ref, tile_ref):
    levels = to_ref.shape[0]
    here = levels // lev_devices
    orders = leg_ref.shape[2]
    rows_here = leg_ref.shape[1] // waves
    lev, wave = lax.axis_index("lev"), lax.axis_index("wave")

    for d in range(lev_devices):

        @pl.when(lev == d)
        def _():
            cols_ref[...] = to_ref[:, d * here : (d + 1) * here]

    cols = split(cols_ref[...])
    eye = lax.broadcasted_iota(jnp.int32, (levels, levels), 0) == lax.broadcasted_iota(
        jnp.int32, (levels, levels), 1
    )
    depth = jnp.sum(jnp.where(eye, depth_ref[...][None, :], 0.0), axis=1, keepdims=True)
    n = lax.broadcasted_iota(jnp.int32, (1, orders), 1)
    nf = n.astype(F32)
    inverse = 1.0 / (1.0 + depth * (nf * (nf + 1.0) / float(orders * orders)))
    keep = n >= ids_ref[wave]
    tiles = orders // 128
    for t in range(tiles):
        tile_ref[t] = leg_ref[0, :, t * 128 : (t + 1) * 128]
    leg = jnp.concatenate(
        [
            jnp.concatenate([tile_ref[t, pl.ds(j, waves, stride=rows_here), :] for t in range(tiles)], 1)
            for j in range(rows_here)
        ],
        0,
    )
    leg = split(jnp.where(keep, leg, 0.0))
    back = split(from_ref[...])

    for c in range(2):
        spec = split(spec_ref[0, :, c, :])
        modes = dot3(cols, spec, ((1,), (0,))) * inverse
        sums = split(dot3(leg, split(modes), ((1,), (1,))))
        four = dot3(sums, back, ((1,), (1,)))
        for d in range(lev_devices):
            for j in range(rows_here):
                out_ref[d * waves : (d + 1) * waves, pl.ds((c * rows_here + j) * here, here)] = four[
                    j * waves : (j + 1) * waves, d * here : (d + 1) * here
                ]


def turn(m, i, p, inv_p):
    x = m * i
    r = x - jnp.floor(x * inv_p) * p
    r = jnp.where(r < 0.0, r + p, r)
    r = jnp.where(r >= p, r - p, r)
    quarter = jnp.floor(4.0 * r * inv_p + 0.5)
    v = (4.0 * r - quarter * p) * ((math.pi / 2) * inv_p)
    s = v * v
    sin = v + v * s * (-1.0 / 6 + s * (1.0 / 120 + s * (-1.0 / 5040 + s * (1.0 / 362880))))
    cos = 1.0 + s * (-0.5 + s * (1.0 / 24 + s * (-1.0 / 720 + s * (1.0 / 40320))))
    odd = (quarter == 1.0) | (quarter == 3.0)
    a, b = jnp.where(odd, sin, cos), jnp.where(odd, cos, sin)
    return (
        jnp.where((quarter == 1.0) | (quarter == 2.0), -a, a),
        jnp.where((quarter == 2.0) | (quarter == 3.0), -b, b),
    )


def grid_kernel(ids_ref, pts_ref, got_ref, out_ref, lhs_ref):
    here, rows_here, lons = out_ref.shape
    waves = ids_ref.shape[0]
    lev_devices = got_ref.shape[0] // waves
    pitch = -(-here // 8) * 8
    chunk = 1280
    starts = list(range(0, lons - chunk // 2, chunk))
    ends = starts[1:] + [lons]
    widest = -(-max(e - s for s, e in zip(starts, ends)) // 128) * 128

    total = got_ref[0:waves, :]
    for d in range(1, lev_devices):
        total = total + got_ref[d * waves : (d + 1) * waves, :]
    row = lax.broadcasted_iota(jnp.int32, (waves, 128), 0)
    m = jnp.zeros((waves, 128), F32)
    for w in range(waves):
        m = jnp.where(row == w, ids_ref[w].astype(F32), m)
    lhs_ref[...] = jnp.zeros_like(lhs_ref)
    lane = lax.broadcasted_iota(jnp.int32, (1, widest), 1).astype(F32)
    points, inner = [], []
    for j in range(rows_here):
        p = pts_ref[j].astype(F32)
        inv_p = 1.0 / jnp.full((1, 1), p, F32)
        mw = m[:, :here]
        weight = jnp.where(2.0 * mw < p, jnp.where(mw == 0.0, 1.0, 2.0), 0.0)
        for c in range(2):
            k, l = (j * 2 + c) * waves, (c * rows_here + j) * here
            part = total[:, l : l + here] * weight
            lhs_ref[k : k + waves, j * pitch : j * pitch + here] = -part if c else part
        points.append((p, inv_p))
        inner.append(turn(m[:, :1], lane, p, inv_p))
    hi, lo = split(lhs_ref[...])
    lhs = jnp.concatenate([hi, hi, lo], 0)
    for start, end in zip(starts, ends):
        size = end - start
        wide = -(-size // 128) * 128
        rows = []
        for j in range(rows_here):
            p, inv_p = points[j]
            ca, sa = turn(m[:, :1], float(start), p, inv_p)
            cb, sb = inner[j][0][:, :wide], inner[j][1][:, :wide]
            inside = lane[:, :wide] < p - float(start)
            rows += [
                jnp.where(inside, ca * cb - sa * sb, 0.0),
                jnp.where(inside, sa * cb + ca * sb, 0.0),
            ]
        hi, lo = split(jnp.concatenate(rows, 0))
        out = lax.dot_general(
            lhs,
            jnp.concatenate([hi, lo, hi], 0),
            (((0,), (0,)), ((), ())),
            preferred_element_type=F32,
        )
        for j in range(rows_here):
            out_ref[:, j, start:end] = out[j * pitch : j * pitch + here, :size]


def on_device(spectral, to_modes, from_modes, mode_depths, legendre, wave_ids, lat_points):
    lev_devices, waves = lax.axis_size("lev"), lax.axis_size("wave")
    here, rows_here = spectral.shape[1], lat_points.shape[0]
    smem = pl.BlockSpec(memory_space=pltpu.SMEM)
    vmem = pl.BlockSpec(memory_space=pltpu.VMEM)
    blocks = pl.pallas_call(
        functools.partial(send_kernel, lev_devices, waves),
        out_shape=jax.ShapeDtypeStruct((lev_devices * waves, 2 * rows_here * here), F32),
        in_specs=[smem] + [vmem] * 5,
        out_specs=vmem,
        scratch_shapes=[
            pltpu.VMEM((to_modes.shape[0], here), F32),
            pltpu.VMEM((legendre.shape[2] // 128, legendre.shape[1], 128), F32),
        ],
        name="send",
    )(wave_ids, spectral, to_modes, from_modes, mode_depths, legendre)
    got = lax.all_to_all(blocks, ("lev", "wave"), 0, 0, tiled=True)
    pitch = -(-here // 8) * 8
    return pl.pallas_call(
        grid_kernel,
        out_shape=jax.ShapeDtypeStruct((here, rows_here, LONS), F32),
        in_specs=[smem, smem, vmem],
        out_specs=vmem,
        scratch_shapes=[pltpu.VMEM((2 * rows_here * waves, rows_here * pitch), F32)],
        name="grid",
    )(wave_ids, lat_points, got)


def solution(mesh):
    return jax.shard_map(
        on_device,
        mesh=mesh,
        in_specs=(
            P("wave", "lev", None, None),
            P(),
            P(),
            P(),
            P("wave", None, None),
            P(),
            P("wave"),
        ),
        out_specs=P("lev", "wave", None),
        check_vma=False,
    )
```

time: 79.7 us -> 23.6 us (0.30)
  local copies, waits for them, and re-layouts: 27.1 us -> 1.39 us
  waiting for transfers between devices: 19.7 us -> 0 us
  blocking collectives: 0 us -> 14.4 us
  starting transfers between devices: 14.3 us -> 0 us
  other arithmetic: 10.3 us -> 0 us
  Pallas kernels: 0 us -> 7.58 us
  loops' own time: 4.04 us -> 0 us
  matrix products: 3.55 us -> 0 us
    all_to_all x3 -> x0, waiting for transfers between devices: 19.7 us -> none  [the longest x1 6.85 us: on_device(): lax.all_to_all(spectral, 'lev', split_axis=3, concat_axis=1, tiled=True)]
    all_to_all x0 -> x1, blocking collectives: none -> 14.4 us  [on_device(): got = lax.all_to_all(blocks, ('lev', 'wave'), 0, 0, tiled=True)]
    all_to_all x3 -> x0, starting transfers between devices: 14.3 us -> none  [the longest x1 6.5 us: on_device(): lax.all_to_all(fourier, 'wave', split_axis=3, concat_axis=1, tiled=True)]
    dynamic_update_slice x4 -> x0, local copies, waits for them, and re-layouts: 12.3 us -> none  [on_device(): lat_rows = lax.map(one_row, (jnp.moveaxis(band_data, 3, 0), lat_points))]
    unnamed x19 -> x1, local copies, waits for them, and re-layouts: 9.8 us -> 0.6 us
    pallas_call x0 -> x2, Pallas kernels: none -> 7.58 us  [the longest x1 4.93 us: on_device(): pl.pallas_call(functools.partial(send_kernel, lev_devices, waves), out_sh...]
    mul x3 -> x0, other arithmetic: 4.69 us -> none  [the longest x2 4.69 us: one_row(): jnp.cos(phases) * weight[:, None]]
    another operation x1 -> x0, loops' own time: 4.04 us -> none  [on_device(): lat_rows = lax.map(one_row, (jnp.moveaxis(band_data, 3, 0), lat_points))]
  transfers between devices with their start and end apart: 3 -> 0, of which waited for: 3 -> 0; matrix products, arithmetic and copies ran while one was open for 2% -> 0% of each run, Pallas kernels for 0% -> 0%
where the time goes in v1:
time: 23.6 us; the launch traced here: 23.3 us
  blocking collectives  14.4 us (61%)
  Pallas kernels  7.58 us (32%)
  local copies, waits for them, and re-layouts  1.39 us (6%)
    all_to_all x1, blocking collectives, on_device(): got = lax.all_to_all(blocks, ('lev', 'wave'), 0, 0, tiled=True)  14.4 us
    pallas_call x1, Pallas kernels, on_device(): pl.pallas_call(functools.partial(send_kernel, lev_devices, waves), out_sh...  4.93 us
    pallas_call x1, Pallas kernels, on_device(): pl.pallas_call(grid_kernel, out_shape=jax.ShapeDtypeStruct((here, rows_he...  2.65 us
    all_to_all x1, local copies, waits for them, and re-layouts, on_device(): got = lax.all_to_all(blocks, ('lev', 'wave'), 0, 0, tiled=True)  0.79 us
    unnamed x1, local copies, waits for them, and re-layouts  0.6 us

profile of v1, /device:TPU:0, one launch (start us, length us, event | category | flops | bytes accessed | tf_op | source)
XLA Modules:
  0.0 23.3 jit_solution(1673588857926850856)
XLA Ops:
  0.0 4.9 %send.1 = f32[32,136]{1,0:T(8,128)} custom-call(s32[8]{0:T(128)} %ids_ref.3, f32[1,34,2,1280]{3,2,1,0:T(2,128)} %spec_ref.1, f32[136,136]{1,0:T(8,128)} %to_ref.1, f32[136,136]{1,0:T(8,128)} %from_ref.1, f32[136]{0:T(256)} %depth_ref.1, f32[1,16,1280]{2,1,0:T(8,128)} %leg_ref.1), custom_call_target="tpu_custom_call" | custom-call | tf_op jit(solution)/shard_map/send/pallas_call | solution.py:154
  4.9 0.8 %copy.8 = f32[32,1,136]{2,1,0:T(1,128)S(1)} copy(f32[32,1,136]{2,0,1:T(8,128)} %bitcast.5) | data formatting | bytes 34816 | tf_op jit(solution)/shard_map/all_to_all | solution.py:165
  5.7 14.4 %all_to_all.11 = f32[32,1,136]{2,1,0:T(1,128)S(1)} all-to-all(f32[32,1,136]{2,1,0:T(1,128)S(1)} %copy.8), channel_id=1, replica_groups=mesh['wave'=8,'lev'=4] {'lev','wave'}, dimensions={0} | all-to-all | bytes 34816 | tf_op jit(solution)/shard_map/all_to_all | solution.py:165
  20.1 0.6 %copy.11 = f32[32,1,136]{2,0,1:T(8,128)} copy(f32[32,1,136]{2,1,0:T(1,128)S(1)} %all_to_all.11) | data formatting | bytes 34816
  20.7 2.6 %grid.1 = f32[34,2,5136]{2,1,0:T(2,128)} custom-call(s32[8]{0:T(128)} %ids_ref.3, s32[2]{0:T(128)} %pts_ref.1, f32[32,136]{1,0:T(8,128)} %bitcast.4), custom_call_target="tpu_custom_call" | custom-call | tf_op jit(solution)/shard_map/grid/pallas_call | solution.py:167

commit v2 on v1

v2 whole, which is shorter than its diff:
```python
import functools
import math

import jax
import jax.numpy as jnp
from jax import lax
from jax.experimental import pallas as pl
from jax.experimental.pallas import tpu as pltpu
from jax.sharding import PartitionSpec as P

LONS = 5136
LANES = 128
CHUNK = 1280
F32, BF16 = jnp.float32, jnp.bfloat16


def up(size, to):
    return -(-size // to) * to


def split(x):
    hi = x.astype(BF16)
    return hi, (x - hi.astype(F32)).astype(BF16)


def dot(a, b, contract):
    return lax.dot_general(a, b, (contract, ((), ())), preferred_element_type=F32)


def send_kernel(
    lev_devices, waves,
    ids_hbm, to_hbm, depth_hbm, leg_hbm, from_hbm, spec_hbm,
    out_ref,
    ids_ref, to_ref, depth_ref, leg_ref, from_ref, spec_ref, cols_ref, tile_ref, back_ref, sems,
):
    copies = [
        pltpu.make_async_copy(source, target, sems.at[i])
        for i, (source, target) in enumerate(
            (
                (spec_hbm, spec_ref),
                (to_hbm, to_ref),
                (depth_hbm, depth_ref),
                (leg_hbm, leg_ref),
                (ids_hbm, ids_ref),
                (from_hbm, from_ref),
            )
        )
    ]
    for copy in copies:
        copy.start()
    levels = to_ref.shape[0]
    here = levels // lev_devices
    orders = leg_ref.shape[2]
    rows_here = leg_ref.shape[1] // waves
    parts = 2 * rows_here
    modes_up, here_up = up(levels, 16), up(here, 16)
    tiles = orders // LANES
    lev, wave = lax.axis_index("lev"), lax.axis_index("wave")
    cols_ref[...] = jnp.zeros_like(cols_ref)
    back_ref[...] = jnp.zeros_like(back_ref)
    tile_ref[...] = jnp.zeros_like(tile_ref)
    for copy in copies[1:]:
        copy.wait()

    for d in range(lev_devices):

        @pl.when(lev == d)
        def _():
            x = to_ref[:, d * here : (d + 1) * here]
            hi = x.astype(BF16).astype(F32)
            cols_ref[:levels, 0:here] = hi
            cols_ref[:levels, here_up : here_up + here] = hi
            cols_ref[:levels, 2 * here_up : 2 * here_up + here] = x - hi

    cols = cols_ref[...].astype(BF16)
    eye = lax.broadcasted_iota(jnp.int32, (levels, levels), 0) == lax.broadcasted_iota(
        jnp.int32, (levels, levels), 1
    )
    depth = jnp.sum(jnp.where(eye, depth_ref[...][None, :], 0.0), axis=1, keepdims=True)
    depth = jnp.concatenate([depth, jnp.zeros((modes_up - levels, 1), F32)], 0)
    n = lax.broadcasted_iota(jnp.int32, (1, orders), 1)
    nf = n.astype(F32)
    inverse = 1.0 / (1.0 + depth * (nf * (nf + 1.0) / float(orders * orders)))
    for t in range(tiles):
        tile_ref[2, t, : leg_ref.shape[1]] = leg_ref[0, :, t * LANES : (t + 1) * LANES]
        for j in range(rows_here):
            x = tile_ref[2, t, pl.ds(j, waves, stride=rows_here), :]
            for c in range(2):
                tile_ref[c, t, pl.ds(c * rows_here + j, waves, stride=parts), :] = x
    keep = n >= ids_ref[wave]
    leg = [
        split(jnp.where(keep, jnp.concatenate([tile_ref[c, t] for t in range(tiles)], 1), 0.0))
        for c in range(2)
    ]
    leg_hi = jnp.concatenate([leg[0][0], leg[1][0]], 1)
    leg_lo = jnp.concatenate([leg[0][1], leg[1][1]], 1)
    leg_both = jnp.concatenate([leg_hi, leg_lo], 0)
    back = from_ref[...].T
    for d in range(lev_devices):
        back_ref[:levels, d * LANES : d * LANES + here] = back[:, d * here : (d + 1) * here]
    back_hi, back_lo = split(back_ref[...])
    back = jnp.concatenate([back_hi, back_lo, back_hi], 0)
    copies[0].wait()

    modes = []
    for c in range(2):
        hi, lo = split(
            jnp.concatenate([spec_ref[0, :, c, :], jnp.zeros((here_up - here, orders), F32)], 0)
        )
        x = dot(cols, jnp.concatenate([hi, lo, hi], 0), ((1,), (0,)))
        modes.append(split(x * inverse))
    hi = jnp.concatenate([modes[0][0], modes[1][0]], 1)
    lo = jnp.concatenate([modes[0][1], modes[1][1]], 1)
    x = dot(hi, leg_both, ((1,), (1,)))
    y = dot(lo, leg_hi, ((1,), (1,)))
    width = parts * waves
    hi, lo = split(x[:, :width] + (x[:, width:] + y))
    four = dot(jnp.concatenate([hi, hi, lo], 0), back, ((0,), (0,)))
    for d in range(lev_devices):
        out_ref[d * width : (d + 1) * width, :] = four[:, d * LANES : (d + 1) * LANES]


def turn(m, i, p, inv_p):
    x = m * i
    r = x - jnp.floor(x * inv_p) * p
    r = jnp.where(r < 0.0, r + p, r)
    r = jnp.where(r >= p, r - p, r)
    quarter = jnp.floor(4.0 * r * inv_p + 0.5)
    v = (4.0 * r - quarter * p) * ((math.pi / 2) * inv_p)
    s = v * v
    sin = v + v * s * (-1.0 / 6 + s * (1.0 / 120 + s * (-1.0 / 5040 + s * (1.0 / 362880))))
    cos = 1.0 + s * (-0.5 + s * (1.0 / 24 + s * (-1.0 / 720 + s * (1.0 / 40320))))
    odd = (quarter == 1.0) | (quarter == 3.0)
    a, b = jnp.where(odd, sin, cos), jnp.where(odd, cos, sin)
    return (
        jnp.where((quarter == 1.0) | (quarter == 2.0), -a, a),
        jnp.where((quarter == 2.0) | (quarter == 3.0), -b, b),
    )


def chunks(lons):
    starts = list(range(0, lons - CHUNK // 2, CHUNK))
    return list(zip(starts, starts[1:] + [lons]))


def table_kernel(ids_hbm, pts_hbm, out_ref, ids_ref, pts_ref, sems):
    copies = [
        pltpu.make_async_copy(ids_hbm, ids_ref, sems.at[0]),
        pltpu.make_async_copy(pts_hbm, pts_ref, sems.at[1]),
    ]
    for copy in copies:
        copy.start()
    for copy in copies:
        copy.wait()
    rows_here = out_ref.shape[0]
    lons = out_ref.shape[3]
    waves = ids_ref.shape[0]
    widest = up(max(end - start for start, end in chunks(lons)), LANES)
    row = lax.broadcasted_iota(jnp.int32, (waves, 1), 0)
    m = jnp.zeros((waves, 1), F32)
    for w in range(waves):
        m = jnp.where(row == w, ids_ref[w].astype(F32), m)
    lane = lax.broadcasted_iota(jnp.int32, (1, widest), 1).astype(F32)
    for j in range(rows_here):
        p = pts_ref[j].astype(F32)
        inv_p = 1.0 / jnp.full((1, 1), p, F32)
        weight = jnp.where(2.0 * m < p, jnp.where(m == 0.0, 1.0, 2.0), 0.0)
        cb, sb = turn(m, lane, p, inv_p)
        for start, end in chunks(lons):
            size = end - start
            ca, sa = turn(m, float(start), p, inv_p)
            ca, sa = ca * weight, sa * weight
            inside = lane < p - float(start)
            cos = jnp.where(inside, ca * cb - sa * sb, 0.0)
            sin = jnp.where(inside, -(sa * cb) - ca * sb, 0.0)
            hi, lo = split(jnp.concatenate([cos, sin], 0))
            out_ref[j, 0, :, start:end] = hi[:, :size]
            out_ref[j, 1, :, start:end] = lo[:, :size]


def grid_kernel(table_ref, got_ref, out_hbm, out_ref, sems):
    here, rows_here, lons = out_ref.shape
    parts = 2 * rows_here
    waves = table_ref.shape[2] // 2
    lev_devices = got_ref.shape[0] // (waves * parts)
    here_up = up(here, 8)
    left = []
    for j in range(rows_here):
        halves = []
        for c in range(2):
            total = None
            for d in range(lev_devices):
                x = got_ref[pl.ds(d * waves * parts + c * rows_here + j, waves, stride=parts), :]
                total = x if total is None else total + x
            halves.append(total)
        hi, lo = split(jnp.concatenate(halves, 0)[:, :here_up])
        left.append(jnp.concatenate([hi, hi, lo], 0))
    copies = []
    for i, (start, end) in enumerate(chunks(lons)):
        for j in range(rows_here):
            hi, lo = table_ref[j, 0, :, start:end], table_ref[j, 1, :, start:end]
            x = dot(left[j], jnp.concatenate([hi, lo, hi], 0), ((0,), (0,)))
            out_ref[:, j, start:end] = x[:here]
        copy = pltpu.make_async_copy(
            out_ref.at[:, :, start:end], out_hbm.at[:, :, start:end], sems.at[i]
        )
        copy.start()
        copies.append(copy)
    for copy in copies:
        copy.wait()


def on_device(spectral, to_modes, from_modes, mode_depths, legendre, wave_ids, lat_points):
    lev_devices, waves = lax.axis_size("lev"), lax.axis_size("wave")
    levels, orders = to_modes.shape[0], spectral.shape[3]
    here, rows_here = spectral.shape[1], lat_points.shape[0]
    parts = 2 * rows_here
    vmem = pl.BlockSpec(memory_space=pltpu.VMEM)
    hbm = pl.BlockSpec(memory_space=pltpu.HBM)
    held = (wave_ids, to_modes, mode_depths, legendre, from_modes, spectral)
    blocks = pl.pallas_call(
        functools.partial(send_kernel, lev_devices, waves),
        out_shape=jax.ShapeDtypeStruct((lev_devices * waves * parts, LANES), F32),
        in_specs=[hbm] * 6,
        out_specs=vmem,
        scratch_shapes=[pltpu.SMEM(wave_ids.shape, jnp.int32)]
        + [pltpu.VMEM(x.shape, F32) for x in held[1:]]
        + [
            pltpu.VMEM((up(levels, 16), 3 * up(here, 16)), F32),
            pltpu.VMEM((3, orders // LANES, parts * waves, LANES), F32),
            pltpu.VMEM((up(levels, 16), lev_devices * LANES), F32),
            pltpu.SemaphoreType.DMA((6,)),
        ],
        compiler_params=pltpu.CompilerParams(vmem_limit_bytes=(8 << 20) + 12 * orders * parts * waves * 4),
        name="send",
    )(*(pltpu.with_memory_space_constraint(x, pltpu.HBM) for x in held))
    got = lax.all_to_all(
        blocks.reshape(lev_devices * waves, parts, LANES), ("lev", "wave"), 0, 0, tiled=True
    ).reshape(blocks.shape)
    table_bytes = rows_here * 4 * waves * up(LONS, LANES) * 2
    table = pl.pallas_call(
        table_kernel,
        out_shape=jax.ShapeDtypeStruct((rows_here, 2, 2 * waves, LONS), BF16),
        in_specs=[hbm, hbm],
        out_specs=vmem,
        scratch_shapes=[
            pltpu.SMEM(wave_ids.shape, jnp.int32),
            pltpu.SMEM(lat_points.shape, jnp.int32),
            pltpu.SemaphoreType.DMA((2,)),
        ],
        compiler_params=pltpu.CompilerParams(vmem_limit_bytes=(8 << 20) + 2 * table_bytes),
        name="table",
    )(*(pltpu.with_memory_space_constraint(x, pltpu.HBM) for x in (wave_ids, lat_points)))
    return pl.pallas_call(
        grid_kernel,
        out_shape=jax.ShapeDtypeStruct((here, rows_here, LONS), F32),
        in_specs=[vmem, vmem],
        out_specs=hbm,
        scratch_shapes=[
            pltpu.VMEM((here, rows_here, LONS), F32),
            pltpu.SemaphoreType.DMA((len(chunks(LONS)),)),
        ],
        compiler_params=pltpu.CompilerParams(vmem_limit_bytes=(8 << 20) + 2 * table_bytes),
        name="grid",
    )(table, got)


def solution(mesh):
    return jax.shard_map(
        on_device,
        mesh=mesh,
        in_specs=(
            P("wave", "lev", None, None),
            P(),
            P(),
            P(),
            P("wave", None, None),
            P(),
            P("wave"),
        ),
        out_specs=P("lev", "wave", None),
        check_vma=False,
    )
```

time: 23.6 us -> 19.6 us (0.83)
  blocking collectives: 14.4 us -> 0 us
  starting transfers between devices: 0 us -> 7.3 us
  waiting for transfers between devices: 0 us -> 6.18 us
  Pallas kernels: 7.58 us -> 5.95 us
  local copies, waits for them, and re-layouts: 1.39 us -> 0 us
    all_to_all x1 -> x0, blocking collectives: 14.4 us -> none  [on_device(): got = lax.all_to_all(blocks, ('lev', 'wave'), 0, 0, tiled=True)]
    all_to_all x0 -> x1, starting transfers between devices: none -> 7.3 us  [on_device(): lax.all_to_all(blocks.reshape(lev_devices * waves, parts, LANES), ('lev',...]
    all_to_all x0 -> x1, waiting for transfers between devices: none -> 6.18 us  [on_device(): lax.all_to_all(blocks.reshape(lev_devices * waves, parts, LANES), ('lev',...]
    pallas_call x1, Pallas kernels: 4.93 us -> 3.47 us  [on_device(): pl.pallas_call(functools.partial(send_kernel, lev_devices, waves), out_sh...]
    pallas_call x1, Pallas kernels: 2.65 us -> 1.4 us  [on_device(): pl.pallas_call(grid_kernel, out_shape=jax.ShapeDtypeStruct((here, rows_he...]
    pallas_call x0 -> x1, Pallas kernels: none -> 1.09 us  [on_device(): pl.pallas_call(table_kernel, out_shape=jax.ShapeDtypeStruct((rows_here, 2...]
    all_to_all x1 -> x0, local copies, waits for them, and re-layouts: 0.79 us -> none  [on_device(): got = lax.all_to_all(blocks, ('lev', 'wave'), 0, 0, tiled=True)]
    unnamed x1 -> x0, local copies, waits for them, and re-layouts: 0.6 us -> none
  transfers between devices with their start and end apart: 0 -> 1, of which waited for: 0 -> 1; matrix products, arithmetic and copies ran while one was open for 0% -> 0% of each run, Pallas kernels for 0% -> 6%
where the time goes in v2:
time: 19.6 us; the launch traced here: 19.5 us
  starting transfers between devices  7.3 us (37%)
  waiting for transfers between devices  6.18 us (32%)
  Pallas kernels  5.95 us (30%)
    all_to_all x1, starting transfers between devices, on_device(): lax.all_to_all(blocks.reshape(lev_devices * waves, parts, LANES), ('lev',...  7.3 us
    all_to_all x1, waiting for transfers between devices, on_device(): lax.all_to_all(blocks.reshape(lev_devices * waves, parts, LANES), ('lev',...  6.18 us
    pallas_call x1, Pallas kernels, on_device(): pl.pallas_call(functools.partial(send_kernel, lev_devices, waves), out_sh...  3.47 us
    pallas_call x1, Pallas kernels, on_device(): pl.pallas_call(grid_kernel, out_shape=jax.ShapeDtypeStruct((here, rows_he...  1.4 us
    pallas_call x1, Pallas kernels, on_device(): pl.pallas_call(table_kernel, out_shape=jax.ShapeDtypeStruct((rows_here, 2...  1.09 us
  transfers between devices with their start and end apart: 1, of which 1 were waited for; matrix products, arithmetic and copies ran while one was open for 0% of the time, Pallas kernels for 6%

profile of v2, /device:TPU:0, one launch (start us, length us, event | category | flops | bytes accessed | tf_op | source)
XLA Modules:
  0.0 19.5 jit_solution(9562475820016238847)
XLA Ops:
  0.0 3.5 %send.1 = f32[128,128]{1,0:T(8,128)} custom-call(s32[8]{0:T(128)} %ids_hbm.3, f32[136,136]{1,0:T(8,128)} %to_hbm.1, f32[136]{0:T(256)} %depth_hbm.1, f32[1,16,1280]{2,1,0:T(8,128)} %leg_hbm.1, f32[136,136]{1,0:T(8,128)} %from_hbm.1, f32[1,34,2,1280]{3,2,1,0:T(2,128)} %spec_hbm.1), custom_call_target="tpu_custom_call" | custom-call | tf_op jit(solution)/shard_map/send/pallas_call | solution.py:221
  3.5 7.3 %all-to-all-start = ((f32[32,4,128]{2,1,0:T(4,128)}), f32[32,4,128]{2,1,0:T(4,128)S(1)}, u32[]{:S(2)}, u32[]{:S(2)}) async-start(f32[32,4,128]{2,1,0:T(4,128)} %bitcast), calls=%async_computation | async-start | bytes 131072 | tf_op jit(solution)/shard_map/all_to_all | solution.py:237
  10.8 1.1 %table.1.table_ref = bf16[2,2,16,5136]{3,2,1,0:T(8,128)(2,1)S(1)} custom-call(s32[8]{0:T(128)} %ids_hbm.3, s32[2]{0:T(128)} %pts_hbm.1), custom_call_target="tpu_custom_call" | custom-call | tf_op jit(solution)/shard_map/table/pallas_call | solution.py:241
  11.9 6.2 %all-to-all-done = f32[32,4,128]{2,1,0:T(4,128)S(1)} async-done(((f32[32,4,128]{2,1,0:T(4,128)}), f32[32,4,128]{2,1,0:T(4,128)S(1)}, u32[]{:S(2)}, u32[]{:S(2)}) %all-to-all-start) | async-done | bytes 65568 | tf_op jit(solution)/shard_map/all_to_all | solution.py:237
  18.1 1.4 %grid.1 = f32[34,2,5136]{2,1,0:T(2,128)} custom-call(bf16[2,2,16,5136]{3,2,1,0:T(8,128)(2,1)S(1)} %table.1.table_ref, f32[128,128]{1,0:T(8,128)S(1)} %bitcast.2), custom_call_target="tpu_custom_call" | custom-call | tf_op jit(solution)/shard_map/grid/pallas_call | solution.py:254
Async XLA Ops:
  3.5 14.6 %all-to-all-start = ((f32[32,4,128]{2,1,0:T(4,128)}), f32[32,4,128]{2,1,0:T(4,128)S(1)}, u32[]{:S(2)}, u32[]{:S(2)}) async-start(f32[32,4,128]{2,1,0:T(4,128)} %bitcast), calls=%async_computation | async-start | bytes 131072 | tf_op jit(solution)/shard_map/all_to_all | solution.py:237

commit v3 on v2

v3 whole, which is shorter than its diff:
```python
import functools
import math

import jax
import jax.numpy as jnp
from jax import lax
from jax.experimental import pallas as pl
from jax.experimental.pallas import tpu as pltpu
from jax.sharding import PartitionSpec as P

LONS = 5136
LANES = 128
CHUNK = 1280
F32, BF16 = jnp.float32, jnp.bfloat16


def up(size, to):
    return -(-size // to) * to


def split(x):
    hi = x.astype(BF16)
    return hi, (x - hi.astype(F32)).astype(BF16)


def dot(a, b, contract):
    return lax.dot_general(a, b, (contract, ((), ())), preferred_element_type=F32)


def turn(m, i, p, inv_p):
    x = m * i
    r = x - jnp.floor(x * inv_p) * p
    r = jnp.where(r < 0.0, r + p, r)
    r = jnp.where(r >= p, r - p, r)
    quarter = jnp.floor(4.0 * r * inv_p + 0.5)
    v = (4.0 * r - quarter * p) * ((math.pi / 2) * inv_p)
    s = v * v
    sin = v + v * s * (-1.0 / 6 + s * (1.0 / 120 + s * (-1.0 / 5040 + s * (1.0 / 362880))))
    cos = 1.0 + s * (-0.5 + s * (1.0 / 24 + s * (-1.0 / 720 + s * (1.0 / 40320))))
    odd = (quarter == 1.0) | (quarter == 3.0)
    a, b = jnp.where(odd, sin, cos), jnp.where(odd, cos, sin)
    return (
        jnp.where((quarter == 1.0) | (quarter == 2.0), -a, a),
        jnp.where((quarter == 2.0) | (quarter == 3.0), -b, b),
    )


def chunks(lons):
    starts = list(range(0, lons - CHUNK // 2, CHUNK))
    return list(zip(starts, starts[1:] + [lons]))


def builds_early():
    return lax.axis_index("wave") < lax.axis_size("wave") // 2


def fetch(pairs, sems, first):
    copies = [pltpu.make_async_copy(a, b, sems.at[first + i]) for i, (a, b) in enumerate(pairs)]
    for copy in copies:
        copy.start()
    for copy in copies:
        copy.wait()


def build_table(ids_ref, pts_ref, table_ref):
    rows_here, lons = table_ref.shape[0], table_ref.shape[3]
    waves = table_ref.shape[2] // 2
    widest = up(max(end - start for start, end in chunks(lons)), LANES)
    row = lax.broadcasted_iota(jnp.int32, (waves, 1), 0)
    m = jnp.zeros((waves, 1), F32)
    for w in range(waves):
        m = jnp.where(row == w, ids_ref[w].astype(F32), m)
    lane = lax.broadcasted_iota(jnp.int32, (1, widest), 1).astype(F32)
    for j in range(rows_here):
        p = pts_ref[j].astype(F32)
        inv_p = 1.0 / jnp.full((1, 1), p, F32)
        weight = jnp.where(2.0 * m < p, jnp.where(m == 0.0, 1.0, 2.0), 0.0)
        cb, sb = turn(m, lane, p, inv_p)
        for start, end in chunks(lons):
            size = end - start
            ca, sa = turn(m, float(start), p, inv_p)
            ca, sa = ca * weight, sa * weight
            inside = lane < p - float(start)
            cos = jnp.where(inside, ca * cb - sa * sb, 0.0)
            sin = jnp.where(inside, -(sa * cb) - ca * sb, 0.0)
            hi, lo = split(jnp.concatenate([cos, sin], 0))
            table_ref[j, 0, :, start:end] = hi[:, :size]
            table_ref[j, 1, :, start:end] = lo[:, :size]


def send_kernel(
    lev_devices, waves,
    ids_hbm, to_hbm, depth_hbm, leg_hbm, from_hbm, spec_hbm, pts_hbm,
    out_ref, table_ref,
    ids_ref, to_ref, depth_ref, leg_ref, from_ref, spec_ref, cols_ref, tile_ref, back_ref, pts_ref, sems,
):
    copies = [
        pltpu.make_async_copy(source, target, sems.at[i])
        for i, (source, target) in enumerate(
            (
                (depth_hbm, depth_ref),
                (to_hbm, to_ref),
                (leg_hbm, leg_ref),
                (ids_hbm, ids_ref),
                (spec_hbm, spec_ref),
                (from_hbm, from_ref),
            )
        )
    ]
    for copy in copies:
        copy.start()
    levels = to_ref.shape[0]
    here = levels // lev_devices
    orders = leg_ref.shape[2]
    rows_here = leg_ref.shape[1] // waves
    parts = 2 * rows_here
    modes_up, here_up = up(levels, 16), up(here, 16)
    tiles = orders // LANES
    lev, wave = lax.axis_index("lev"), lax.axis_index("wave")
    cols_ref[...] = jnp.zeros_like(cols_ref)
    back_ref[...] = jnp.zeros_like(back_ref)
    tile_ref[...] = jnp.zeros_like(tile_ref)
    copies[0].wait()

    eye = lax.broadcasted_iota(jnp.int32, (levels, levels), 0) == lax.broadcasted_iota(
        jnp.int32, (levels, levels), 1
    )
    depth = jnp.sum(jnp.where(eye, depth_ref[...][None, :], 0.0), axis=1, keepdims=True)
    depth = jnp.concatenate([depth, jnp.zeros((modes_up - levels, 1), F32)], 0)
    n = lax.broadcasted_iota(jnp.int32, (1, orders), 1)
    nf = n.astype(F32)
    inverse = 1.0 / (1.0 + depth * (nf * (nf + 1.0) / float(orders * orders)))
    copies[1].wait()
    for d in range(lev_devices):

        @pl.when(lev == d)
        def _():
            x = to_ref[:, d * here : (d + 1) * here]
            hi = x.astype(BF16).astype(F32)
            cols_ref[:levels, 0:here] = hi
            cols_ref[:levels, here_up : here_up + here] = hi
            cols_ref[:levels, 2 * here_up : 2 * here_up + here] = x - hi

    cols = cols_ref[...].astype(BF16)
    copies[2].wait()
    copies[3].wait()
    for t in range(tiles):
        tile_ref[2, t, : leg_ref.shape[1]] = leg_ref[0, :, t * LANES : (t + 1) * LANES]
        for j in range(rows_here):
            x = tile_ref[2, t, pl.ds(j, waves, stride=rows_here), :]
            for c in range(2):
                tile_ref[c, t, pl.ds(c * rows_here + j, waves, stride=parts), :] = x
    keep = n >= ids_ref[wave]
    leg = [
        split(jnp.where(keep, jnp.concatenate([tile_ref[c, t] for t in range(tiles)], 1), 0.0))
        for c in range(2)
    ]
    leg_hi = jnp.concatenate([leg[0][0], leg[1][0]], 1)
    leg_lo = jnp.concatenate([leg[0][1], leg[1][1]], 1)
    leg_both = jnp.concatenate([leg_hi, leg_lo], 0)

    @pl.when(builds_early())
    def _():
        fetch(((pts_hbm, pts_ref),), sems, 6)
        build_table(ids_ref, pts_ref, table_ref)

    copies[4].wait()
    modes = []
    for c in range(2):
        hi, lo = split(
            jnp.concatenate([spec_ref[0, :, c, :], jnp.zeros((here_up - here, orders), F32)], 0)
        )
        x = dot(cols, jnp.concatenate([hi, lo, hi], 0), ((1,), (0,)))
        modes.append(split(x * inverse))
    copies[5].wait()
    back = from_ref[...].T
    for d in range(lev_devices):
        back_ref[:levels, d * LANES : d * LANES + here] = back[:, d * here : (d + 1) * here]
    back_hi, back_lo = split(back_ref[...])
    back = jnp.concatenate([back_hi, back_lo, back_hi], 0)
    hi = jnp.concatenate([modes[0][0], modes[1][0]], 1)
    lo = jnp.concatenate([modes[0][1], modes[1][1]], 1)
    x = dot(hi, leg_both, ((1,), (1,)))
    y = dot(lo, leg_hi, ((1,), (1,)))
    width = parts * waves
    hi, lo = split(x[:, :width] + (x[:, width:] + y))
    four = dot(jnp.concatenate([hi, hi, lo], 0), back, ((0,), (0,)))
    for d in range(lev_devices):
        out_ref[d * width : (d + 1) * width, :] = four[:, d * LANES : (d + 1) * LANES]


def grid_kernel(first_ref, got_ref, ids_hbm, pts_hbm, out_hbm, out_ref, table_ref, ids_ref, pts_ref, sems):
    early = builds_early()

    @pl.when(early)
    def _():
        table_ref[...] = first_ref[...]

    @pl.when(jnp.logical_not(early))
    def _():
        fetch(((ids_hbm, ids_ref), (pts_hbm, pts_ref)), sems, 0)
        build_table(ids_ref, pts_ref, table_ref)

    here, rows_here, lons = out_ref.shape
    parts = 2 * rows_here
    waves = table_ref.shape[2] // 2
    lev_devices = got_ref.shape[0] // (waves * parts)
    here_up = up(here, 8)
    left = []
    for j in range(rows_here):
        halves = []
        for c in range(2):
            total = None
            for d in range(lev_devices):
                x = got_ref[pl.ds(d * waves * parts + c * rows_here + j, waves, stride=parts), :]
                total = x if total is None else total + x
            halves.append(total)
        hi, lo = split(jnp.concatenate(halves, 0)[:, :here_up])
        left.append(jnp.concatenate([hi, hi, lo], 0))
    copies = []
    for i, (start, end) in enumerate(chunks(lons)):
        for j in range(rows_here):
            hi, lo = table_ref[j, 0, :, start:end], table_ref[j, 1, :, start:end]
            x = dot(left[j], jnp.concatenate([hi, lo, hi], 0), ((0,), (0,)))
            out_ref[:, j, start:end] = x[:here]
        copy = pltpu.make_async_copy(
            out_ref.at[:, :, start:end], out_hbm.at[:, :, start:end], sems.at[i]
        )
        copy.start()
        copies.append(copy)
    for copy in copies:
        copy.wait()


def on_device(spectral, to_modes, from_modes, mode_depths, legendre, wave_ids, lat_points):
    lev_devices, waves = lax.axis_size("lev"), lax.axis_size("wave")
    levels, orders = to_modes.shape[0], spectral.shape[3]
    here, rows_here = spectral.shape[1], lat_points.shape[0]
    parts = 2 * rows_here
    vmem, hbm = pl.BlockSpec(memory_space=pltpu.VMEM), pl.BlockSpec(memory_space=pl.ANY)
    table = jax.ShapeDtypeStruct((rows_here, 2, 2 * waves, LONS), BF16)
    table_bytes = table.size * 2
    spectral, to_modes, from_modes, mode_depths, legendre, wave_ids, lat_points = (
        pltpu.with_memory_space_constraint(x, pltpu.HBM)
        for x in (spectral, to_modes, from_modes, mode_depths, legendre, wave_ids, lat_points)
    )
    ids = [pltpu.SMEM(wave_ids.shape, jnp.int32), pltpu.SMEM(lat_points.shape, jnp.int32)]
    held = (to_modes, mode_depths, legendre, from_modes, spectral)
    blocks, first = pl.pallas_call(
        functools.partial(send_kernel, lev_devices, waves),
        out_shape=(jax.ShapeDtypeStruct((lev_devices * waves * parts, LANES), F32), table),
        in_specs=[hbm] * 7,
        out_specs=(vmem, vmem),
        scratch_shapes=[ids[0]]
        + [pltpu.VMEM(x.shape, F32) for x in held]
        + [
            pltpu.VMEM((up(levels, 16), 3 * up(here, 16)), F32),
            pltpu.VMEM((3, orders // LANES, parts * waves, LANES), F32),
            pltpu.VMEM((up(levels, 16), lev_devices * LANES), F32),
            ids[1],
            pltpu.SemaphoreType.DMA((7,)),
        ],
        compiler_params=pltpu.CompilerParams(
            vmem_limit_bytes=(8 << 20) + 12 * orders * parts * waves * 4 + 2 * table_bytes
        ),
        name="send",
    )(wave_ids, *held, lat_points)
    got = lax.all_to_all(
        blocks.reshape(lev_devices * waves, parts, LANES), ("lev", "wave"), 0, 0, tiled=True
    ).reshape(blocks.shape)
    return pl.pallas_call(
        grid_kernel,
        out_shape=jax.ShapeDtypeStruct((here, rows_here, LONS), F32),
        in_specs=[vmem, vmem, hbm, hbm],
        out_specs=hbm,
        scratch_shapes=[
            pltpu.VMEM((here, rows_here, LONS), F32),
            pltpu.VMEM(table.shape, BF16),
            *ids,
            pltpu.SemaphoreType.DMA((max(2, len(chunks(LONS))),)),
        ],
        compiler_params=pltpu.CompilerParams(vmem_limit_bytes=(8 << 20) + 3 * table_bytes),
        name="grid",
    )(first, got, wave_ids, lat_points)


def solution(mesh):
    return jax.shard_map(
        on_device,
        mesh=mesh,
        in_specs=(
            P("wave", "lev", None, None),
            P(),
            P(),
            P(),
            P("wave", None, None),
            P(),
            P("wave"),
        ),
        out_specs=P("lev", "wave", None),
        check_vma=False,
    )
```

time: 19.6 us -> 18.5 us (0.944)
  blocking collectives: 0 us -> 13.3 us
  starting transfers between devices: 7.3 us -> 0 us
  waiting for transfers between devices: 6.18 us -> 0 us
  Pallas kernels: 5.95 us -> 4.95 us
    all_to_all x0 -> x1, blocking collectives: none -> 13.3 us  [on_device(): lax.all_to_all(blocks.reshape(lev_devices * waves, parts, LANES), ('lev',...]
    all_to_all x1 -> x0, starting transfers between devices: 7.3 us -> none  [on_device(): lax.all_to_all(blocks.reshape(lev_devices * waves, parts, LANES), ('lev',...]
    all_to_all x1 -> x0, waiting for transfers between devices: 6.18 us -> none  [on_device(): lax.all_to_all(blocks.reshape(lev_devices * waves, parts, LANES), ('lev',...]
    pallas_call x1 -> x0, Pallas kernels: 1.09 us -> none  [on_device(): pl.pallas_call(table_kernel, out_shape=jax.ShapeDtypeStruct((rows_here, 2...]
  transfers between devices with their start and end apart: 1 -> 0, of which waited for: 1 -> 0; matrix products, arithmetic and copies ran while one was open for 0% -> 0% of each run, Pallas kernels for 6% -> 0%
where the time goes in v3:
time: 18.5 us; the launch traced here: 18.3 us
  blocking collectives  13.3 us (72%)
  Pallas kernels  4.95 us (27%)
    all_to_all x1, blocking collectives, on_device(): lax.all_to_all(blocks.reshape(lev_devices * waves, parts, LANES), ('lev',...  13.3 us
    pallas_call x1, Pallas kernels, on_device(): pl.pallas_call(functools.partial(send_kernel, lev_devices, waves), out_sh...  3.51 us
    pallas_call x1, Pallas kernels, on_device(): pl.pallas_call(grid_kernel, out_shape=jax.ShapeDtypeStruct((here, rows_he...  1.44 us

profile of v3, /device:TPU:0, one launch (start us, length us, event | category | flops | bytes accessed | tf_op | source)
XLA Modules:
  0.0 18.3 jit_solution(1465463838724380979)
XLA Ops:
  0.0 3.5 %send.1 = (f32[128,128]{1,0:T(8,128)S(1)}, bf16[2,2,16,5136]{3,2,1,0:T(8,128)(2,1)S(1)}) custom-call(s32[8]{0:T(128)} %ids_hbm.3, f32[136,136]{1,0:T(8,128)} %to_hbm.1, f32[136]{0:T(256)} %depth_hbm.1, f32[1,16,1280]{2,1,0:T(8,128)} %leg_hbm.1, f32[136,136]{1,0:T(8,128)} %from_hbm.1, f32[1,34,2,1280]{3,2,1,0:T(2,128)} %spec_hbm.1, s32[2]{0:T(128)} %pts_hbm.3), custom_call_target="tpu_custom_call" | custom-call | tf_op jit(solution)/shard_map/send/pallas_call | solution.py:249
  3.5 13.3 %all_to_all.5 = f32[32,4,128]{2,1,0:T(4,128)S(1)} all-to-all(f32[32,4,128]{2,1,0:T(4,128)S(1)} %bitcast.3), channel_id=1, replica_groups=mesh['wave'=8,'lev'=4] {'lev','wave'}, dimensions={0} | all-to-all | bytes 131072 | tf_op jit(solution)/shard_map/all_to_all | solution.py:268
  16.8 1.4 %grid.1 = f32[34,2,5136]{2,1,0:T(2,128)} custom-call(bf16[2,2,16,5136]{3,2,1,0:T(8,128)(2,1)S(1)} %get-tuple-element.7.first_ref, f32[128,128]{1,0:T(8,128)S(1)} %bitcast.2, s32[8]{0:T(128)} %ids_hbm.3, s32[2]{0:T(128)} %pts_hbm.3), custom_call_target="tpu_custom_call" | custom-call | tf_op jit(solution)/shard_map/grid/pallas_call | solution.py:271

commit v4 on v3

--- a/solution.py
+++ b/solution.py
@@ -11,6 +11,7 @@
 LONS = 5136
 LANES = 128
 CHUNK = 1280
+FIRST = 640
 F32, BF16 = jnp.float32, jnp.bfloat16
 
 
@@ -45,8 +46,10 @@
     )
 
 
-def chunks(lons):
+def chunks(lons, first=0):
     starts = list(range(0, lons - CHUNK // 2, CHUNK))
+    if first:
+        starts.insert(1, first)
     return list(zip(starts, starts[1:] + [lons]))
 
 
@@ -91,8 +94,8 @@
 def send_kernel(
     lev_devices, waves,
     ids_hbm, to_hbm, depth_hbm, leg_hbm, from_hbm, spec_hbm, pts_hbm,
-    out_ref, table_ref,
-    ids_ref, to_ref, depth_ref, leg_ref, from_ref, spec_ref, cols_ref, tile_ref, back_ref, pts_ref, sems,
+    out_ref, table_ref, limit_ref, grid_hbm,
+    ids_ref, to_ref, depth_ref, leg_ref, from_ref, spec_ref, cols_ref, tile_ref, back_ref, pts_ref, zero_ref, sems,
 ):
     copies = [
         pltpu.make_async_copy(source, target, sems.at[i])
@@ -159,9 +162,25 @@
     leg_lo = jnp.concatenate([leg[0][1], leg[1][1]], 1)
     leg_both = jnp.concatenate([leg_hi, leg_lo], 0)
 
-    @pl.when(builds_early())
+    early = builds_early()
+    lons = table_ref.shape[3]
+    clears = [
+        pltpu.make_async_copy(
+            zero_ref.at[:, :, : end - start], grid_hbm.at[:, :, start:end], sems.at[7 + i]
+        )
+        for i, (start, end) in enumerate(chunks(lons))
+    ]
+
+    @pl.when(early)
     def _():
+        zero_ref[...] = jnp.zeros_like(zero_ref)
+        for clear in clears:
+            clear.start()
         fetch(((pts_hbm, pts_ref),), sems, 6)
+        longest = pts_ref[0]
+        for j in range(1, rows_here):
+            longest = jnp.maximum(longest, pts_ref[j])
+        limit_ref[...] = jnp.full(limit_ref.shape, longest, jnp.int32).astype(F32)
         build_table(ids_ref, pts_ref, table_ref)
 
     copies[4].wait()
@@ -188,48 +207,78 @@
     for d in range(lev_devices):
         out_ref[d * width : (d + 1) * width, :] = four[:, d * LANES : (d + 1) * LANES]
 
-
-def grid_kernel(first_ref, got_ref, ids_hbm, pts_hbm, out_hbm, out_ref, table_ref, ids_ref, pts_ref, sems):
-    early = builds_early()
-
     @pl.when(early)
     def _():
-        table_ref[...] = first_ref[...]
-
-    @pl.when(jnp.logical_not(early))
-    def _():
-        fetch(((ids_hbm, ids_ref), (pts_hbm, pts_ref)), sems, 0)
-        build_table(ids_ref, pts_ref, table_ref)
-
+        for clear in clears:
+            clear.wait()
+
+
+def grid_kernel(
+    first_ref, limit_ref, got_ref, ids_hbm, pts_hbm, cleared_hbm,
+    out_hbm,
+    out_ref, table_ref, ids_ref, pts_ref, sems,
+):
     here, rows_here, lons = out_ref.shape
     parts = 2 * rows_here
     waves = table_ref.shape[2] // 2
     lev_devices = got_ref.shape[0] // (waves * parts)
     here_up = up(here, 8)
-    left = []
-    for j in range(rows_here):
-        halves = []
-        for c in range(2):
-            total = None
-            for d in range(lev_devices):
-                x = got_ref[pl.ds(d * waves * parts + c * rows_here + j, waves, stride=parts), :]
-                total = x if total is None else total + x
-            halves.append(total)
-        hi, lo = split(jnp.concatenate(halves, 0)[:, :here_up])
-        left.append(jnp.concatenate([hi, hi, lo], 0))
-    copies = []
-    for i, (start, end) in enumerate(chunks(lons)):
+    early = builds_early()
+
+    def left_sides():
+        left = []
         for j in range(rows_here):
-            hi, lo = table_ref[j, 0, :, start:end], table_ref[j, 1, :, start:end]
+            halves = []
+            for c in range(2):
+                total = None
+                for d in range(lev_devices):
+                    x = got_ref[pl.ds(d * waves * parts + c * rows_here + j, waves, stride=parts), :]
+                    total = x if total is None else total + x
+                halves.append(total)
+            hi, lo = split(jnp.concatenate(halves, 0)[:, :here_up])
+            left.append(jnp.concatenate([hi, hi, lo], 0))
+        return left
+
+    def fill(ref, left, start, end):
+        for j in range(rows_here):
+            hi, lo = ref[j, 0, :, start:end], ref[j, 1, :, start:end]
             x = dot(left[j], jnp.concatenate([hi, lo, hi], 0), ((0,), (0,)))
             out_ref[:, j, start:end] = x[:here]
-        copy = pltpu.make_async_copy(
+
+    def copy(i, start, end):
+        return pltpu.make_async_copy(
             out_ref.at[:, :, start:end], out_hbm.at[:, :, start:end], sems.at[i]
         )
-        copy.start()
-        copies.append(copy)
-    for copy in copies:
-        copy.wait()
+
+    @pl.when(early)
+    def _():
+        left = left_sides()
+        limit = jnp.max(limit_ref[...]).astype(jnp.int32)
+        parts_of = chunks(lons, FIRST)
+        for i, (start, end) in enumerate(parts_of):
+
+            def one():
+                fill(first_ref, left, start, end)
+                copy(i, start, end).start()
+
+            one() if i == 0 else pl.when(start < limit)(one)
+        for i, (start, end) in enumerate(parts_of):
+
+            def done():
+                copy(i, start, end).wait()
+
+            done() if i == 0 else pl.when(start < limit)(done)
+
+    @pl.when(jnp.logical_not(early))
+    def _():
+        fetch(((ids_hbm, ids_ref), (pts_hbm, pts_ref)), sems, 0)
+        build_table(ids_ref, pts_ref, table_ref)
+        left = left_sides()
+        for i, (start, end) in enumerate(chunks(lons)):
+            fill(table_ref, left, start, end)
+            copy(i, start, end).start()
+        for i, (start, end) in enumerate(chunks(lons)):
+            copy(i, start, end).wait()
 
 
 def on_device(spectral, to_modes, from_modes, mode_depths, legendre, wave_ids, lat_points):
@@ -244,13 +293,20 @@
         pltpu.with_memory_space_constraint(x, pltpu.HBM)
         for x in (spectral, to_modes, from_modes, mode_depths, legendre, wave_ids, lat_points)
     )
+    widest = max(end - start for start, end in chunks(LONS))
     ids = [pltpu.SMEM(wave_ids.shape, jnp.int32), pltpu.SMEM(lat_points.shape, jnp.int32)]
     held = (to_modes, mode_depths, legendre, from_modes, spectral)
-    blocks, first = pl.pallas_call(
+    grid = jax.ShapeDtypeStruct((here, rows_here, LONS), F32)
+    blocks, first, limit, cleared = pl.pallas_call(
         functools.partial(send_kernel, lev_devices, waves),
-        out_shape=(jax.ShapeDtypeStruct((lev_devices * waves * parts, LANES), F32), table),
+        out_shape=(
+            jax.ShapeDtypeStruct((lev_devices * waves * parts, LANES), F32),
+            table,
+            jax.ShapeDtypeStruct((8, LANES), F32),
+            grid,
+        ),
         in_specs=[hbm] * 7,
-        out_specs=(vmem, vmem),
+        out_specs=(vmem, vmem, vmem, hbm),
         scratch_shapes=[ids[0]]
         + [pltpu.VMEM(x.shape, F32) for x in held]
         + [
@@ -258,7 +314,8 @@
             pltpu.VMEM((3, orders // LANES, parts * waves, LANES), F32),
             pltpu.VMEM((up(levels, 16), lev_devices * LANES), F32),
             ids[1],
-            pltpu.SemaphoreType.DMA((7,)),
+            pltpu.VMEM((here, rows_here, widest), F32),
+            pltpu.SemaphoreType.DMA((7 + len(chunks(LONS)),)),
         ],
         compiler_params=pltpu.CompilerParams(
             vmem_limit_bytes=(8 << 20) + 12 * orders * parts * waves * 4 + 2 * table_bytes
@@ -270,18 +327,19 @@
     ).reshape(blocks.shape)
     return pl.pallas_call(
         grid_kernel,
-        out_shape=jax.ShapeDtypeStruct((here, rows_here, LONS), F32),
-        in_specs=[vmem, vmem, hbm, hbm],
+        out_shape=grid,
+        in_specs=[vmem, vmem, vmem, hbm, hbm, hbm],
+        input_output_aliases={5: 0},
         out_specs=hbm,
         scratch_shapes=[
             pltpu.VMEM((here, rows_here, LONS), F32),
             pltpu.VMEM(table.shape, BF16),
             *ids,
-            pltpu.SemaphoreType.DMA((max(2, len(chunks(LONS))),)),
+            pltpu.SemaphoreType.DMA((len(chunks(LONS, FIRST)),)),
         ],
         compiler_params=pltpu.CompilerParams(vmem_limit_bytes=(8 << 20) + 3 * table_bytes),
         name="grid",
-    )(first, got, wave_ids, lat_points)
+    )(first, limit, got, wave_ids, lat_points, cleared)
 
 
 def solution(mesh):

time: 18.5 us -> 18.2 us (0.984)
  Pallas kernels: 4.95 us -> 4.71 us
    pallas_call x1, Pallas kernels: 1.44 us -> 1.13 us  [on_device(): pl.pallas_call(grid_kernel, out_shape=grid, in_specs=[vmem, vmem, vmem, h...]
where the time goes in v4:
time: 18.2 us; the launch traced here: 18 us
  blocking collectives  13.3 us (73%)
  Pallas kernels  4.71 us (26%)
    all_to_all x1, blocking collectives, on_device(): lax.all_to_all(blocks.reshape(lev_devices * waves, parts, LANES), ('lev',...  13.3 us
    pallas_call x1, Pallas kernels, on_device(): pl.pallas_call(functools.partial(send_kernel, lev_devices, waves), out_sh...  3.58 us
    pallas_call x1, Pallas kernels, on_device(): pl.pallas_call(grid_kernel, out_shape=grid, in_specs=[vmem, vmem, vmem, h...  1.13 us

profile of v4, /device:TPU:0, one launch (start us, length us, event | category | flops | bytes accessed | tf_op | source)
XLA Modules:
  0.0 18.0 jit_solution(7658987615595948680)
XLA Ops:
  0.0 3.6 %send.1 = (f32[128,128]{1,0:T(8,128)S(1)}, bf16[2,2,16,5136]{3,2,1,0:T(8,128)(2,1)S(1)}, f32[8,128]{1,0:T(8,128)S(1)}, f32[34,2,5136]{2,1,0:T(2,128)}) custom-call(s32[8]{0:T(128)} %ids_hbm.3, f32[136,136]{1,0:T(8,128)} %to_hbm.1, f32[136]{0:T(256)} %depth_hbm.1, f32[1,16,1280]{2,1,0:T(8,128)} %leg_hbm.1, f32[136,136]{1,0:T(8,128)} %from_hbm.1, ...), custom_call_target="tpu_custom_call" | custom-call | tf_op jit(solution)/shard_map/send/pallas_call | solution.py:300
  3.6 13.3 %all_to_all.5 = f32[32,4,128]{2,1,0:T(4,128)S(1)} all-to-all(f32[32,4,128]{2,1,0:T(4,128)S(1)} %bitcast.3), channel_id=1, replica_groups=mesh['wave'=8,'lev'=4] {'lev','wave'}, dimensions={0} | all-to-all | bytes 131072 | tf_op jit(solution)/shard_map/all_to_all | solution.py:325
  16.9 1.1 %grid.1 = f32[34,2,5136]{2,1,0:T(2,128)} custom-call(bf16[2,2,16,5136]{3,2,1,0:T(8,128)(2,1)S(1)} %get-tuple-element.9.first_ref, f32[8,128]{1,0:T(8,128)S(1)} %get-tuple-element.10.limit_ref, f32[128,128]{1,0:T(8,128)S(1)} %bitcast.2, s32[8]{0:T(128)} %ids_hbm.3, s32[2]{0:T(128)} %pts_hbm.3, ...), custom_call_target="tpu_custom_call", output_to_operand_aliasing={{}: (5, {})} | custom-call | tf_op jit(solution)/shard_map/grid/pallas_call | solution.py:328

commit v5 on v4

--- a/solution.py
+++ b/solution.py
@@ -12,6 +12,7 @@
 LANES = 128
 CHUNK = 1280
 FIRST = 640
+TAILS = (2, 5)
 F32, BF16 = jnp.float32, jnp.bfloat16
 
 
@@ -54,7 +55,7 @@
 
 
 def builds_early():
-    return lax.axis_index("wave") < lax.axis_size("wave") // 2
+    return lax.axis_index("wave") < lax.axis_size("wave") // 4
 
 
 def fetch(pairs, sems, first):
@@ -118,7 +119,6 @@
     rows_here = leg_ref.shape[1] // waves
     parts = 2 * rows_here
     modes_up, here_up = up(levels, 16), up(here, 16)
-    tiles = orders // LANES
     lev, wave = lax.axis_index("lev"), lax.axis_index("wave")
     cols_ref[...] = jnp.zeros_like(cols_ref)
     back_ref[...] = jnp.zeros_like(back_ref)
@@ -130,9 +130,6 @@
     )
     depth = jnp.sum(jnp.where(eye, depth_ref[...][None, :], 0.0), axis=1, keepdims=True)
     depth = jnp.concatenate([depth, jnp.zeros((modes_up - levels, 1), F32)], 0)
-    n = lax.broadcasted_iota(jnp.int32, (1, orders), 1)
-    nf = n.astype(F32)
-    inverse = 1.0 / (1.0 + depth * (nf * (nf + 1.0) / float(orders * orders)))
     copies[1].wait()
     for d in range(lev_devices):
 
@@ -144,23 +141,9 @@
             cols_ref[:levels, here_up : here_up + here] = hi
             cols_ref[:levels, 2 * here_up : 2 * here_up + here] = x - hi
 
-    cols = cols_ref[...].astype(BF16)
     copies[2].wait()
     copies[3].wait()
-    for t in range(tiles):
-        tile_ref[2, t, : leg_ref.shape[1]] = leg_ref[0, :, t * LANES : (t + 1) * LANES]
-        for j in range(rows_here):
-            x = tile_ref[2, t, pl.ds(j, waves, stride=rows_here), :]
-            for c in range(2):
-                tile_ref[c, t, pl.ds(c * rows_here + j, waves, stride=parts), :] = x
-    keep = n >= ids_ref[wave]
-    leg = [
-        split(jnp.where(keep, jnp.concatenate([tile_ref[c, t] for t in range(tiles)], 1), 0.0))
-        for c in range(2)
-    ]
-    leg_hi = jnp.concatenate([leg[0][0], leg[1][0]], 1)
-    leg_lo = jnp.concatenate([leg[0][1], leg[1][1]], 1)
-    leg_both = jnp.concatenate([leg_hi, leg_lo], 0)
+    own = ids_ref[wave]
 
     early = builds_early()
     lons = table_ref.shape[3]
@@ -183,29 +166,52 @@
         limit_ref[...] = jnp.full(limit_ref.shape, longest, jnp.int32).astype(F32)
         build_table(ids_ref, pts_ref, table_ref)
 
-    copies[4].wait()
-    modes = []
-    for c in range(2):
-        hi, lo = split(
-            jnp.concatenate([spec_ref[0, :, c, :], jnp.zeros((here_up - here, orders), F32)], 0)
-        )
-        x = dot(cols, jnp.concatenate([hi, lo, hi], 0), ((1,), (0,)))
-        modes.append(split(x * inverse))
-    copies[5].wait()
-    back = from_ref[...].T
-    for d in range(lev_devices):
-        back_ref[:levels, d * LANES : d * LANES + here] = back[:, d * here : (d + 1) * here]
-    back_hi, back_lo = split(back_ref[...])
-    back = jnp.concatenate([back_hi, back_lo, back_hi], 0)
-    hi = jnp.concatenate([modes[0][0], modes[1][0]], 1)
-    lo = jnp.concatenate([modes[0][1], modes[1][1]], 1)
-    x = dot(hi, leg_both, ((1,), (1,)))
-    y = dot(lo, leg_hi, ((1,), (1,)))
-    width = parts * waves
-    hi, lo = split(x[:, :width] + (x[:, width:] + y))
-    four = dot(jnp.concatenate([hi, hi, lo], 0), back, ((0,), (0,)))
-    for d in range(lev_devices):
-        out_ref[d * width : (d + 1) * width, :] = four[:, d * LANES : (d + 1) * LANES]
+    def solve(low):
+        tiles = range(low // LANES, orders // LANES)
+        n = low + lax.broadcasted_iota(jnp.int32, (1, orders - low), 1)
+        nf = n.astype(F32)
+        inverse = 1.0 / (1.0 + depth * (nf * (nf + 1.0) / float(orders * orders)))
+        cols = cols_ref[...].astype(BF16)
+        for t in tiles:
+            tile_ref[2, t, : leg_ref.shape[1]] = leg_ref[0, :, t * LANES : (t + 1) * LANES]
+            for j in range(rows_here):
+                x = tile_ref[2, t, pl.ds(j, waves, stride=rows_here), :]
+                for c in range(2):
+                    tile_ref[c, t, pl.ds(c * rows_here + j, waves, stride=parts), :] = x
+        keep = n >= own
+        leg = [
+            split(jnp.where(keep, jnp.concatenate([tile_ref[c, t] for t in tiles], 1), 0.0))
+            for c in range(2)
+        ]
+        leg_hi = jnp.concatenate([leg[0][0], leg[1][0]], 1)
+        leg_lo = jnp.concatenate([leg[0][1], leg[1][1]], 1)
+        leg_both = jnp.concatenate([leg_hi, leg_lo], 0)
+        copies[4].wait()
+        modes = []
+        for c in range(2):
+            zero = jnp.zeros((here_up - here, orders - low), F32)
+            hi, lo = split(jnp.concatenate([spec_ref[0, :, c, low:], zero], 0))
+            x = dot(cols, jnp.concatenate([hi, lo, hi], 0), ((1,), (0,)))
+            modes.append(split(x * inverse))
+        copies[5].wait()
+        back = from_ref[...].T
+        for d in range(lev_devices):
+            back_ref[:levels, d * LANES : d * LANES + here] = back[:, d * here : (d + 1) * here]
+        back_hi, back_lo = split(back_ref[...])
+        back = jnp.concatenate([back_hi, back_lo, back_hi], 0)
+        hi = jnp.concatenate([modes[0][0], modes[1][0]], 1)
+        lo = jnp.concatenate([modes[0][1], modes[1][1]], 1)
+        x = dot(hi, leg_both, ((1,), (1,)))
+        y = dot(lo, leg_hi, ((1,), (1,)))
+        width = parts * waves
+        hi, lo = split(x[:, :width] + (x[:, width:] + y))
+        four = dot(jnp.concatenate([hi, hi, lo], 0), back, ((0,), (0,)))
+        for d in range(lev_devices):
+            out_ref[d * width : (d + 1) * width, :] = four[:, d * LANES : (d + 1) * LANES]
+
+    lows = [0] + [orders - up(orders // share, LANES) for share in TAILS]
+    for low, above in zip(lows, lows[1:] + [orders]):
+        pl.when((own >= low) & (own < above))(functools.partial(solve, low))
 
     @pl.when(early)
     def _():

time: 18.2 us -> 17.7 us (0.973)
  blocking collectives: 13.3 us -> 12.8 us
    all_to_all x1, blocking collectives: 13.3 us -> 12.8 us  [on_device(): lax.all_to_all(blocks.reshape(lev_devices * waves, parts, LANES), ('lev',...]
where the time goes in v5:
time: 17.7 us; the launch traced here: 17.4 us
  blocking collectives  12.8 us (72%)
  Pallas kernels  4.6 us (26%)
    all_to_all x1, blocking collectives, on_device(): lax.all_to_all(blocks.reshape(lev_devices * waves, parts, LANES), ('lev',...  12.8 us
    pallas_call x1, Pallas kernels, on_device(): pl.pallas_call(functools.partial(send_kernel, lev_devices, waves), out_sh...  3.65 us
    pallas_call x1, Pallas kernels, on_device(): pl.pallas_call(grid_kernel, out_shape=grid, in_specs=[vmem, vmem, vmem, h...  0.95 us

profile of v5, /device:TPU:0, one launch (start us, length us, event | category | flops | bytes accessed | tf_op | source)
XLA Modules:
  0.0 17.4 jit_solution(8637031724866629339)
XLA Ops:
  0.0 3.7 %send.1 = (f32[128,128]{1,0:T(8,128)S(1)}, bf16[2,2,16,5136]{3,2,1,0:T(8,128)(2,1)S(1)}, f32[8,128]{1,0:T(8,128)S(1)}, f32[34,2,5136]{2,1,0:T(2,128)}) custom-call(s32[8]{0:T(128)} %ids_hbm.3, f32[136,136]{1,0:T(8,128)} %to_hbm.1, f32[136]{0:T(256)} %depth_hbm.1, f32[1,16,1280]{2,1,0:T(8,128)} %leg_hbm.1, f32[136,136]{1,0:T(8,128)} %from_hbm.1, ...), custom_call_target="tpu_custom_call" | custom-call | tf_op jit(solution)/shard_map/send/pallas_call | solution.py:306
  3.7 12.8 %all_to_all.5 = f32[32,4,128]{2,1,0:T(4,128)S(1)} all-to-all(f32[32,4,128]{2,1,0:T(4,128)S(1)} %bitcast.3), channel_id=1, replica_groups=mesh['wave'=8,'lev'=4] {'lev','wave'}, dimensions={0} | all-to-all | bytes 131072 | tf_op jit(solution)/shard_map/all_to_all | solution.py:331
  16.4 0.9 %grid.1 = f32[34,2,5136]{2,1,0:T(2,128)} custom-call(bf16[2,2,16,5136]{3,2,1,0:T(8,128)(2,1)S(1)} %get-tuple-element.9.first_ref, f32[8,128]{1,0:T(8,128)S(1)} %get-tuple-element.10.limit_ref, f32[128,128]{1,0:T(8,128)S(1)} %bitcast.2, s32[8]{0:T(128)} %ids_hbm.3, s32[2]{0:T(128)} %pts_hbm.3, ...), custom_call_target="tpu_custom_call", output_to_operand_aliasing={{}: (5, {})} | custom-call | tf_op jit(solution)/shard_map/grid/pallas_call | solution.py:334

commit v6 on v5

--- a/solution.py
+++ b/solution.py
@@ -11,8 +11,9 @@
 LONS = 5136
 LANES = 128
 CHUNK = 1280
-FIRST = 640
-TAILS = (2, 5)
+FIRST = 1024
+TAILS = (5, 4, 3, 2, 1)
+SHORT = 512
 F32, BF16 = jnp.float32, jnp.bfloat16
 
 
@@ -185,7 +186,6 @@
         ]
         leg_hi = jnp.concatenate([leg[0][0], leg[1][0]], 1)
         leg_lo = jnp.concatenate([leg[0][1], leg[1][1]], 1)
-        leg_both = jnp.concatenate([leg_hi, leg_lo], 0)
         copies[4].wait()
         modes = []
         for c in range(2):
@@ -198,18 +198,28 @@
         for d in range(lev_devices):
             back_ref[:levels, d * LANES : d * LANES + here] = back[:, d * here : (d + 1) * here]
         back_hi, back_lo = split(back_ref[...])
-        back = jnp.concatenate([back_hi, back_lo, back_hi], 0)
         hi = jnp.concatenate([modes[0][0], modes[1][0]], 1)
         lo = jnp.concatenate([modes[0][1], modes[1][1]], 1)
-        x = dot(hi, leg_both, ((1,), (1,)))
-        y = dot(lo, leg_hi, ((1,), (1,)))
         width = parts * waves
-        hi, lo = split(x[:, :width] + (x[:, width:] + y))
-        four = dot(jnp.concatenate([hi, hi, lo], 0), back, ((0,), (0,)))
+        if orders - low <= SHORT:
+            x = dot(
+                jnp.concatenate([leg_hi, leg_lo, leg_hi], 1),
+                jnp.concatenate([hi, hi, lo], 1),
+                ((1,), (1,)),
+            )
+            hi, lo = split(x)
+            x = dot(jnp.concatenate([hi, lo], 0), back_hi, ((1,), (0,)))
+            four = x[:width] + (x[width:] + dot(hi, back_lo, ((1,), (0,))))
+        else:
+            x = dot(hi, jnp.concatenate([leg_hi, leg_lo], 0), ((1,), (1,)))
+            y = dot(lo, leg_hi, ((1,), (1,)))
+            hi, lo = split(x[:, :width] + (x[:, width:] + y))
+            back = jnp.concatenate([back_hi, back_lo, back_hi], 0)
+            four = dot(jnp.concatenate([hi, hi, lo], 0), back, ((0,), (0,)))
         for d in range(lev_devices):
             out_ref[d * width : (d + 1) * width, :] = four[:, d * LANES : (d + 1) * LANES]
 
-    lows = [0] + [orders - up(orders // share, LANES) for share in TAILS]
+    lows = [0] + [orders - up(orders * tenths // 10, LANES) for tenths in TAILS]
     for low, above in zip(lows, lows[1:] + [orders]):
         pl.when((own >= low) & (own < above))(functools.partial(solve, low))
 

time: 17.7 us -> 17.5 us (0.989)
  no operation moved by 1% of the time
where the time goes in v6:
time: 17.5 us; the launch traced here: 17.3 us
  blocking collectives  12.7 us (73%)
  Pallas kernels  4.65 us (27%)
    all_to_all x1, blocking collectives, on_device(): lax.all_to_all(blocks.reshape(lev_devices * waves, parts, LANES), ('lev',...  12.7 us
    pallas_call x1, Pallas kernels, on_device(): pl.pallas_call(functools.partial(send_kernel, lev_devices, waves), out_sh...  3.65 us
    pallas_call x1, Pallas kernels, on_device(): pl.pallas_call(grid_kernel, out_shape=grid, in_specs=[vmem, vmem, vmem, h...  1 us

profile of v6, /device:TPU:0, one launch (start us, length us, event | category | flops | bytes accessed | tf_op | source)
XLA Modules:
  0.0 17.3 jit_solution(6208969750302354250)
XLA Ops:
  0.0 3.7 %send.1 = (f32[128,128]{1,0:T(8,128)S(1)}, bf16[2,2,16,5136]{3,2,1,0:T(8,128)(2,1)S(1)}, f32[8,128]{1,0:T(8,128)S(1)}, f32[34,2,5136]{2,1,0:T(2,128)}) custom-call(s32[8]{0:T(128)} %ids_hbm.3, f32[136,136]{1,0:T(8,128)} %to_hbm.1, f32[136]{0:T(256)} %depth_hbm.1, f32[1,16,1280]{2,1,0:T(8,128)} %leg_hbm.1, f32[136,136]{1,0:T(8,128)} %from_hbm.1, ...), custom_call_target="tpu_custom_call" | custom-call | tf_op jit(solution)/shard_map/send/pallas_call | solution.py:316
  3.7 12.7 %all_to_all.5 = f32[32,4,128]{2,1,0:T(4,128)S(1)} all-to-all(f32[32,4,128]{2,1,0:T(4,128)S(1)} %bitcast.3), channel_id=1, replica_groups=mesh['wave'=8,'lev'=4] {'lev','wave'}, dimensions={0} | all-to-all | bytes 131072 | tf_op jit(solution)/shard_map/all_to_all | solution.py:341
  16.3 1.0 %grid.1 = f32[34,2,5136]{2,1,0:T(2,128)} custom-call(bf16[2,2,16,5136]{3,2,1,0:T(8,128)(2,1)S(1)} %get-tuple-element.9.first_ref, f32[8,128]{1,0:T(8,128)S(1)} %get-tuple-element.10.limit_ref, f32[128,128]{1,0:T(8,128)S(1)} %bitcast.2, s32[8]{0:T(128)} %ids_hbm.3, s32[2]{0:T(128)} %pts_hbm.3, ...), custom_call_target="tpu_custom_call", output_to_operand_aliasing={{}: (5, {})} | custom-call | tf_op jit(solution)/shard_map/grid/pallas_call | solution.py:344

commit v7 on v6

--- a/solution.py
+++ b/solution.py
@@ -178,7 +178,7 @@
             for j in range(rows_here):
                 x = tile_ref[2, t, pl.ds(j, waves, stride=rows_here), :]
                 for c in range(2):
-                    tile_ref[c, t, pl.ds(c * rows_here + j, waves, stride=parts), :] = x
+                    tile_ref[c, t, pl.ds(j * 2 * waves + c, waves, stride=2), :] = x
         keep = n >= own
         leg = [
             split(jnp.where(keep, jnp.concatenate([tile_ref[c, t] for t in tiles], 1), 0.0))
@@ -216,8 +216,14 @@
             hi, lo = split(x[:, :width] + (x[:, width:] + y))
             back = jnp.concatenate([back_hi, back_lo, back_hi], 0)
             four = dot(jnp.concatenate([hi, hi, lo], 0), back, ((0,), (0,)))
+        rows = 2 * waves
+        message = four[:rows]
+        for j in range(1, rows_here):
+            message = message + pltpu.roll(
+                four[j * rows : (j + 1) * rows], j * (LANES // rows_here), 1
+            )
         for d in range(lev_devices):
-            out_ref[d * width : (d + 1) * width, :] = four[:, d * LANES : (d + 1) * LANES]
+            out_ref[d * rows : (d + 1) * rows, :] = message[:, d * LANES : (d + 1) * LANES]
 
     lows = [0] + [orders - up(orders * tenths // 10, LANES) for tenths in TAILS]
     for low, above in zip(lows, lows[1:] + [orders]):
@@ -235,23 +241,24 @@
     out_ref, table_ref, ids_ref, pts_ref, sems,
 ):
     here, rows_here, lons = out_ref.shape
-    parts = 2 * rows_here
     waves = table_ref.shape[2] // 2
-    lev_devices = got_ref.shape[0] // (waves * parts)
+    lev_devices = got_ref.shape[0] // (waves * 2)
     here_up = up(here, 8)
     early = builds_early()
 
     def left_sides():
+        halves = []
+        for c in range(2):
+            total = None
+            for d in range(lev_devices):
+                x = got_ref[pl.ds((d * waves) * 2 + c, waves, stride=2), :]
+                total = x if total is None else total + x
+            halves.append(total)
+        both = jnp.concatenate(halves, 0)
         left = []
         for j in range(rows_here):
-            halves = []
-            for c in range(2):
-                total = None
-                for d in range(lev_devices):
-                    x = got_ref[pl.ds(d * waves * parts + c * rows_here + j, waves, stride=parts), :]
-                    total = x if total is None else total + x
-                halves.append(total)
-            hi, lo = split(jnp.concatenate(halves, 0)[:, :here_up])
+            pitch = j * (LANES // rows_here)
+            hi, lo = split(both[:, pitch : pitch + here_up])
             left.append(jnp.concatenate([hi, hi, lo], 0))
         return left
 
@@ -301,6 +308,7 @@
     lev_devices, waves = lax.axis_size("lev"), lax.axis_size("wave")
     levels, orders = to_modes.shape[0], spectral.shape[3]
     here, rows_here = spectral.shape[1], lat_points.shape[0]
+    assert up(here, 8) * rows_here <= LANES
     parts = 2 * rows_here
     vmem, hbm = pl.BlockSpec(memory_space=pltpu.VMEM), pl.BlockSpec(memory_space=pl.ANY)
     table = jax.ShapeDtypeStruct((rows_here, 2, 2 * waves, LONS), BF16)
@@ -316,7 +324,7 @@
     blocks, first, limit, cleared = pl.pallas_call(
         functools.partial(send_kernel, lev_devices, waves),
         out_shape=(
-            jax.ShapeDtypeStruct((lev_devices * waves * parts, LANES), F32),
+            jax.ShapeDtypeStruct((lev_devices * waves * 2, LANES), F32),
             table,
             jax.ShapeDtypeStruct((8, LANES), F32),
             grid,
@@ -339,7 +347,7 @@
         name="send",
     )(wave_ids, *held, lat_points)
     got = lax.all_to_all(
-        blocks.reshape(lev_devices * waves, parts, LANES), ("lev", "wave"), 0, 0, tiled=True
+        blocks.reshape(lev_devices * waves, 2, LANES), ("lev", "wave"), 0, 0, tiled=True
     ).reshape(blocks.shape)
     return pl.pallas_call(
         grid_kernel,

time: 17.5 us -> 17.5 us (level)
  no operation moved by 1% of the time
where the time goes in v7:
time: 17.5 us; the launch traced here: 17.4 us
  blocking collectives  12.6 us (72%)
  Pallas kernels  4.78 us (27%)
    all_to_all x1, blocking collectives, on_device(): lax.all_to_all(blocks.reshape(lev_devices * waves, 2, LANES), ('lev', 'wa...  12.6 us
    pallas_call x1, Pallas kernels, on_device(): pl.pallas_call(functools.partial(send_kernel, lev_devices, waves), out_sh...  3.73 us
    pallas_call x1, Pallas kernels, on_device(): pl.pallas_call(grid_kernel, out_shape=grid, in_specs=[vmem, vmem, vmem, h...  1.05 us

profile of v7, /device:TPU:0, one launch (start us, length us, event | category | flops | bytes accessed | tf_op | source)
XLA Modules:
  0.0 17.4 jit_solution(10832231003646256165)
XLA Ops:
  0.0 3.7 %send.1 = (f32[64,128]{1,0:T(8,128)S(1)}, bf16[2,2,16,5136]{3,2,1,0:T(8,128)(2,1)S(1)}, f32[8,128]{1,0:T(8,128)S(1)}, f32[34,2,5136]{2,1,0:T(2,128)}) custom-call(s32[8]{0:T(128)} %ids_hbm.3, f32[136,136]{1,0:T(8,128)} %to_hbm.1, f32[136]{0:T(256)} %depth_hbm.1, f32[1,16,1280]{2,1,0:T(8,128)} %leg_hbm.1, f32[136,136]{1,0:T(8,128)} %from_hbm.1, ...), custom_call_target="tpu_custom_call" | custom-call | tf_op jit(solution)/shard_map/send/pallas_call | solution.py:324
  3.7 12.6 %all_to_all.5 = f32[32,2,128]{2,1,0:T(2,128)S(1)} all-to-all(f32[32,2,128]{2,1,0:T(2,128)S(1)} %bitcast.3), channel_id=1, replica_groups=mesh['wave'=8,'lev'=4] {'lev','wave'}, dimensions={0} | all-to-all | bytes 65536 | tf_op jit(solution)/shard_map/all_to_all | solution.py:349
  16.3 1.0 %grid.1 = f32[34,2,5136]{2,1,0:T(2,128)} custom-call(bf16[2,2,16,5136]{3,2,1,0:T(8,128)(2,1)S(1)} %get-tuple-element.9.first_ref, f32[8,128]{1,0:T(8,128)S(1)} %get-tuple-element.10.limit_ref, f32[64,128]{1,0:T(8,128)S(1)} %bitcast.2, s32[8]{0:T(128)} %ids_hbm.3, s32[2]{0:T(128)} %pts_hbm.3, ...), custom_call_target="tpu_custom_call", output_to_operand_aliasing={{}: (5, {})} | custom-call | tf_op jit(solution)/shard_map/grid/pallas_call | solution.py:352

commit v8 on v6

--- a/solution.py
+++ b/solution.py
@@ -12,6 +12,7 @@
 LANES = 128
 CHUNK = 1280
 FIRST = 1024
+HEAD = 2
 TAILS = (5, 4, 3, 2, 1)
 SHORT = 512
 F32, BF16 = jnp.float32, jnp.bfloat16
@@ -269,21 +270,28 @@
     @pl.when(early)
     def _():
         left = left_sides()
+        pieces = chunks(lons, FIRST)
+        first = pieces[0][1]
+        cuts = [(i * first // HEAD, (i + 1) * first // HEAD) for i in range(HEAD)]
+        for i, (start, end) in enumerate(cuts):
+            fill(first_ref, left, start, end)
+            copy(i, start, end).start()
         limit = jnp.max(limit_ref[...]).astype(jnp.int32)
-        parts_of = chunks(lons, FIRST)
-        for i, (start, end) in enumerate(parts_of):
-
-            def one():
-                fill(first_ref, left, start, end)
-                copy(i, start, end).start()
-
-            one() if i == 0 else pl.when(start < limit)(one)
-        for i, (start, end) in enumerate(parts_of):
-
-            def done():
-                copy(i, start, end).wait()
-
-            done() if i == 0 else pl.when(start < limit)(done)
+
+        @pl.when(first < limit)
+        def _():
+            for i, (start, end) in enumerate(pieces[1:], HEAD):
+
+                def one():
+                    fill(first_ref, left, start, end)
+                    copy(i, start, end).start()
+
+                pl.when(start < limit)(one)
+            for i, (start, end) in enumerate(pieces[1:], HEAD):
+                pl.when(start < limit)(copy(i, start, end).wait)
+
+        for i, (start, end) in enumerate(cuts):
+            copy(i, start, end).wait()
 
     @pl.when(jnp.logical_not(early))
     def _():
@@ -351,7 +359,7 @@
             pltpu.VMEM((here, rows_here, LONS), F32),
             pltpu.VMEM(table.shape, BF16),
             *ids,
-            pltpu.SemaphoreType.DMA((len(chunks(LONS, FIRST)),)),
+            pltpu.SemaphoreType.DMA((len(chunks(LONS, FIRST)) + HEAD,)),
         ],
         compiler_params=pltpu.CompilerParams(vmem_limit_bytes=(8 << 20) + 3 * table_bytes),
         name="grid",

time: 17.5 us -> 17.5 us (level)
  no operation moved by 1% of the time
where the time goes in v8:
time: 17.5 us; the launch traced here: 17.3 us
  blocking collectives  12.7 us (73%)
  Pallas kernels  4.63 us (26%)
    all_to_all x1, blocking collectives, on_device(): lax.all_to_all(blocks.reshape(lev_devices * waves, parts, LANES), ('lev',...  12.7 us
    pallas_call x1, Pallas kernels, on_device(): pl.pallas_call(functools.partial(send_kernel, lev_devices, waves), out_sh...  3.65 us
    pallas_call x1, Pallas kernels, on_device(): pl.pallas_call(grid_kernel, out_shape=grid, in_specs=[vmem, vmem, vmem, h...  0.98 us

profile of v8, /device:TPU:0, one launch (start us, length us, event | category | flops | bytes accessed | tf_op | source)
XLA Modules:
  0.0 17.3 jit_solution(12290282997908927208)
XLA Ops:
  0.0 3.7 %send.1 = (f32[128,128]{1,0:T(8,128)S(1)}, bf16[2,2,16,5136]{3,2,1,0:T(8,128)(2,1)S(1)}, f32[8,128]{1,0:T(8,128)S(1)}, f32[34,2,5136]{2,1,0:T(2,128)}) custom-call(s32[8]{0:T(128)} %ids_hbm.3, f32[136,136]{1,0:T(8,128)} %to_hbm.1, f32[136]{0:T(256)} %depth_hbm.1, f32[1,16,1280]{2,1,0:T(8,128)} %leg_hbm.1, f32[136,136]{1,0:T(8,128)} %from_hbm.1, ...), custom_call_target="tpu_custom_call" | custom-call | tf_op jit(solution)/shard_map/send/pallas_call | solution.py:324
  3.7 12.7 %all_to_all.5 = f32[32,4,128]{2,1,0:T(4,128)S(1)} all-to-all(f32[32,4,128]{2,1,0:T(4,128)S(1)} %bitcast.3), channel_id=1, replica_groups=mesh['wave'=8,'lev'=4] {'lev','wave'}, dimensions={0} | all-to-all | bytes 131072 | tf_op jit(solution)/shard_map/all_to_all | solution.py:349
  16.3 1.0 %grid.1 = f32[34,2,5136]{2,1,0:T(2,128)} custom-call(bf16[2,2,16,5136]{3,2,1,0:T(8,128)(2,1)S(1)} %get-tuple-element.9.first_ref, f32[8,128]{1,0:T(8,128)S(1)} %get-tuple-element.10.limit_ref, f32[128,128]{1,0:T(8,128)S(1)} %bitcast.2, s32[8]{0:T(128)} %ids_hbm.3, s32[2]{0:T(128)} %pts_hbm.3, ...), custom_call_target="tpu_custom_call", output_to_operand_aliasing={{}: (5, {})} | custom-call | tf_op jit(solution)/shard_map/grid/pallas_call | solution.py:352
